TPU v7x, 32 devices: a whole 2x2x4 slice. The times are simulated.
32 devices in a mesh: groups: 2 (over x), gz: 16 (over z, y, core).
Axes of the slice: x: 2, y: 2, z: 4, core: 2. Of those that a mesh axis runs over, the one named last changes fastest.
Arguments:
- estimate: float32 [16, 512, 256], P(None, 'gz', 'groups'), parts along dimension 2, may hold values from 0 to 2
- frames: int32 [3, 5, 16, 512, 256], P(None, None, 'gz', None, 'groups'), parts along dimension 4, may hold values from 0 to 4095
- phase_index: int32 [3, 5], replicated, may hold values from 0 to 4, each once within a row
- axial_otf: float32 [3, 2, 16], replicated, may hold values from -4 to 4
- row_blur: float32 [3, 128, 128], replicated, may hold values from -0.5 to 0.5
- column_taps: float32 [3, 7], replicated, may hold values from 0.1 to 1
Outputs:
- gradient: float32 [16, 512, 256], P(None, 'gz', 'groups'), parts along dimension 2
There are 2 independent parts, one for each index of `groups`. A program takes and returns all parts, laid end to end along the dimension named above; an argument that names none is the same for every part. Nothing has to cross between parts.
Inputs may be any that keep to these rules, and one draw needn't show every extreme that they name: `phase_index`: for each orientation the 5 frames take every phase step once.
All inputs are finite; a program needn't handle non-finite values.
Results may differ from a plain program's by a relative error of at most 0.0001.
Values sent between devices are 32-bit elements; how exact they have to be, the bound alone decides.
No kernel may reach another device: no remote copies, remote signals or barrier semaphores. Data moves between devices by JAX's collectives and lax.ppermute only.
A program may use at most 64 MiB of HBM per device.

v0:
```python
import math

import jax
import jax.numpy as jnp
import numpy as np
from jax import lax
from jax.experimental import pallas as pl
from jax.experimental.pallas import tpu as pltpu
from jax.sharding import PartitionSpec as P


pattern_period = 3.7
orient_base = 0.3
data_scale = 1.0 / 1024.0
PAD = 8


def exact_dot(left_side, right_side):
    return jnp.dot(
        left_side, right_side, preferred_element_type=jnp.float32, precision=lax.Precision.HIGHEST
    )


def split(values):
    high = values.astype(jnp.bfloat16)
    low = (values - high.astype(jnp.float32)).astype(jnp.bfloat16)
    return high, low


def wide(values):
    high, low = split(values)
    return jnp.concatenate([high, low], axis=1)


def weights(matrix):
    row = wide(matrix)
    return jnp.concatenate([row, row], axis=0)


def narrow(product):
    half = product.shape[1] // 2
    return product[:, :half] + product[:, half:]


def wide_dot(left_side, right_side):
    return jnp.dot(left_side, right_side, preferred_element_type=jnp.float32)


def pattern_table(orients, loop_width, row_count, pad):
    columns = np.arange(-pad, loop_width + pad) % loop_width
    rows = np.arange(row_count)
    images = []
    for orient in range(orients):
        direction = orient_base + 2.0 * math.pi * orient / 3.0
        phase = (
            columns.astype(np.float32)[:, None] * np.float32(math.cos(direction))
            + rows.astype(np.float32)[None, :] * np.float32(math.sin(direction))
        ) * np.float32(2.0 * math.pi / pattern_period)
        images += [np.cos(phase.astype(np.float64)), np.sin(phase.astype(np.float64))]
    return np.stack(images).astype(np.float32)


def harmonic_of(cos_one, sin_one, harmonic):
    if harmonic == 1:
        return cos_one, sin_one
    return cos_one * cos_one - sin_one * sin_one, 2.0 * (sin_one * cos_one)


def blurred(mixed, image, taps, begin, step):
    reach = (len(taps) - 1) // 2
    acc = None
    for offset in range(-reach, reach + 1):
        term = taps[offset + reach] * mixed[image, pl.ds(begin + PAD - offset, step), :]
        acc = term if acc is None else acc + term
    return acc


def band_rows(mixed, images, taps, table, weight, band, begin, step):
    at = pl.ds(begin + (table.shape[1] - mixed.shape[1]) // 2 + PAD, step)
    parts = [wide(blurred(mixed, image, cut, begin, step)) for image, cut in zip(images, taps)]
    product = narrow(wide_dot(jnp.concatenate(parts, axis=0), weight))
    acc = None
    for orient in range(len(images) // 2):
        cos_pattern, sin_pattern = harmonic_of(
            table[2 * orient, at, :], table[2 * orient + 1, at, :], band
        )
        even = product[2 * orient * step : (2 * orient + 1) * step]
        odd = product[(2 * orient + 1) * step : (2 * orient + 2) * step]
        term = cos_pattern * even - sin_pattern * odd
        acc = term if acc is None else acc + term
    return acc


def put(out, index, band, values):
    width = out.shape[3]
    cores = out.shape[1]
    shares = values.shape[0] // width
    for share in range(shares):
        rows = values[share * width : (share + 1) * width]
        out[index * (shares // cores) + share // cores, share % cores, band] = rows


def scaled_taps(taps_ref, band, scale):
    return [taps_ref[band, at] * scale for at in range(taps_ref.shape[1])]


def data_kernel(
    phase_hbm, taps_hbm, frames_hbm, blur_hbm, table_hbm, *refs,
):
    targets, scratch = refs[:-12], refs[-12:]
    raw, summed, mixed, weight, table, blur_rows, out, phase_ref, taps_ref = scratch[:9]
    frame_sems, side_sems, out_sems = scratch[9:]

    orients, phases = raw.shape[0], raw.shape[1]
    loop_width = raw.shape[2]
    bands = out.shape[2]
    core = lax.axis_index("gz") % 2
    phase_copy = pltpu.make_async_copy(phase_hbm, phase_ref, side_sems.at[0])
    phase_copy.start()
    copies = []
    for orient in range(orients):
        row = []
        for index in range(phases):
            copy = pltpu.make_async_copy(
                frames_hbm.at[orient, index, 0],
                raw.at[orient, index],
                frame_sems.at[orient, index],
            )
            copy.start()
            row.append(copy)
        copies.append(row)
    taps_copy = pltpu.make_async_copy(taps_hbm, taps_ref, side_sems.at[1])
    taps_copy.start()
    blur_copy = pltpu.make_async_copy(blur_hbm, blur_rows, side_sems.at[2])
    blur_copy.start()
    table_copy = pltpu.make_async_copy(table_hbm, table, side_sems.at[3])
    table_copy.start()
    step = loop_width // 2
    reach = (taps_ref.shape[1] - 1) // 2
    total = 4 * orients
    count = orients * phases
    first_sine, second_sine = math.sin(2 * math.pi / 5), math.sin(4 * math.pi / 5)
    ratio = second_sine / first_sine
    phase_copy.wait()
    for orient in range(orients):
        holder = []
        for step_index in range(phases):
            at_step = 0
            for index in range(1, phases):
                at_step = jnp.where(phase_ref[orient, index] == step_index, index, at_step)
            holder.append(at_step)
        for copy in copies[orient]:
            copy.wait()

        def mix(index, carry):
            rows = pl.ds(pl.multiple_of(index * step, step), step)
            at = pl.ds(pl.multiple_of(index * step + PAD, 8), step)
            f0, f1, f2, f3, f4 = [raw[orient, k, rows, :] for k in holder]
            near, far, near_odd, far_odd = f1 + f4, f2 + f3, f1 - f4, f2 - f3
            both = near + far
            even = (4 * f0 - both).astype(jnp.float32)
            swing = (near - far).astype(jnp.float32) * math.sqrt(5.0)
            near_odd = near_odd.astype(jnp.float32)
            far_odd = far_odd.astype(jnp.float32)
            mixed[2 * orient, at, :] = even + swing
            mixed[2 * orient + 1, at, :] = near_odd + ratio * far_odd
            mixed[2 * (orients + orient), at, :] = even - swing
            mixed[2 * (orients + orient) + 1, at, :] = ratio * near_odd - far_odd
            plain = f0 + both
            if orient:
                plain = plain + summed[rows, :]
            if orient < orients - 1:
                summed[rows, :] = plain
            else:
                mixed[total, at, :] = plain.astype(jnp.float32) * data_scale - 2.0 * count
            return carry

        lax.fori_loop(0, loop_width // step, mix, 0)
    for image in range(total + 1):
        mixed[image, PAD - reach : PAD, :] = mixed[
            image, loop_width + PAD - reach : loop_width + PAD, :
        ]
        mixed[image, loop_width + PAD : loop_width + PAD + reach, :] = mixed[
            image, PAD : PAD + reach, :
        ]
    taps_copy.wait()
    blur_copy.wait()
    for band in range(bands):
        weight[band] = weights(blur_rows[band])
    even_scale, odd_scale = data_scale / (4.0 * count), data_scale * first_sine / count
    taps = [scaled_taps(taps_ref, 0, 1.0 / count)]
    for band in range(1, bands):
        taps.append(
            [scaled_taps(taps_ref, band, even_scale), scaled_taps(taps_ref, band, odd_scale)]
            * orients
        )

    def plain_out(index, carry):
        begin = pl.multiple_of(index * step, step)
        rows = blurred(mixed, total, taps[0], begin, step)
        put(out, index, 0, narrow(wide_dot(wide(rows), weight[0])))
        return carry

    lax.fori_loop(0, loop_width // step, plain_out, 0)
    out_copies = []

    def ship(band):
        for at, target in enumerate(targets):
            half = (core + at) % 2 if len(targets) > 1 else 0
            copy = pltpu.make_async_copy(
                out.at[:, half, band], target.at[:, band], out_sems.at[at, band]
            )
            copy.start()
            out_copies.append(copy)

    ship(0)
    table_copy.wait()
    for band in range(1, bands):
        images = list(range(2 * orients * (band - 1), 2 * orients * band))

        def band_out(index, carry):
            begin = pl.multiple_of(index * step, step)
            put(
                out,
                index,
                band,
                band_rows(mixed, images, taps[band], table, weight[band], band, begin, step),
            )
            return carry

        lax.fori_loop(0, loop_width // step, band_out, 0)
        ship(band)
    for copy in out_copies:
        copy.wait()


def data_sums(frames, phase_index, row_blur, column_taps, table, chunks, cores):
    orients, phases, _, loop_width, row_count = frames.shape
    bands = row_blur.shape[0]
    width = loop_width // chunks
    anywhere = pl.BlockSpec(memory_space=pltpu.HBM)
    return pl.pallas_call(
        data_kernel,
        out_shape=[
            jax.ShapeDtypeStruct((chunks // cores, bands, width, row_count), jnp.float32)
        ]
        * cores,
        in_specs=[anywhere] * 5,
        out_specs=[anywhere] * cores,
        scratch_shapes=[
            pltpu.VMEM((orients, phases, loop_width, row_count), jnp.int32),
            pltpu.VMEM((loop_width, row_count), jnp.int32),
            pltpu.VMEM((4 * orients + 1, loop_width + 2 * PAD, row_count), jnp.float32),
            pltpu.VMEM((bands, 2 * row_count, 2 * row_count), jnp.bfloat16),
            pltpu.VMEM(table.shape, jnp.float32),
            pltpu.VMEM(row_blur.shape, jnp.float32),
            pltpu.VMEM((chunks // cores, cores, bands, width, row_count), jnp.float32),
            pltpu.SMEM(phase_index.shape, jnp.int32),
            pltpu.SMEM(column_taps.shape, jnp.float32),
            pltpu.SemaphoreType.DMA((orients, phases)),
            pltpu.SemaphoreType.DMA((4,)),
            pltpu.SemaphoreType.DMA((cores, bands)),
        ],
        cost_estimate=pl.CostEstimate(
            flops=13 * loop_width * 2 * 256 * 256, bytes_accessed=frames.size * 4, transcendentals=0
        ),
        compiler_params=pltpu.CompilerParams(vmem_limit_bytes=63 << 20),
        name="data_sums",
    )(phase_index, column_taps, frames, row_blur, table)


def estimate_kernel(taps_ref, axial_ref, table_hbm, blur_ref, out_ref, table_ref, sem):
    width = out_ref.shape[0]
    source = table_hbm
    if table_hbm.shape != table_ref.shape:
        begin = pl.multiple_of(lax.axis_index("gz") * width, 8)
        source = table_hbm.at[:, pl.ds(begin, table_ref.shape[1]), :]
    table_copy = pltpu.make_async_copy(source, table_ref, sem)
    table_copy.start()
    bands, _, planes, _ = axial_ref.shape
    orients = table_ref.shape[0] // 2
    reach = (taps_ref.shape[1] - 1) // 2
    span = 2 * reach
    step = max(d for d in range(1, 23) if out_ref.shape[0] % d == 0 and (d == 1 or d * planes <= 352))

    def lags_of(band, scale):
        return [
            scale
            * sum(
                taps_ref[band, d] * taps_ref[band, d + shift]
                for d in range(0, 2 * reach + 1 - shift)
            )
            for shift in range(span + 1)
        ]

    def filtered(columns, lags):
        rows = []
        for i in range(step):
            acc = lags[0] * columns[i + span]
            for shift in range(1, span + 1):
                acc = acc + lags[shift] * (columns[i + span - shift] + columns[i + span + shift])
            rows.append(wide(acc))
        return rows

    def weight_of(band):
        matrix = blur_ref[band]
        return weights(
            lax.dot_general(
                matrix,
                matrix,
                (((0,), (0,)), ((), ())),
                preferred_element_type=jnp.float32,
                precision=lax.Precision.HIGHEST,
            )
        )

    weight = [weight_of(band) for band in range(bands)]
    shift = PAD - span
    table_copy.wait()
    lags = [lags_of(0, 1.0)] + [lags_of(band, 0.5 / orients) for band in range(1, bands)]

    def chunk(index, carry):
        begin = index * step
        rows = filtered([axial_ref[0, begin + i] for i in range(step + 2 * span)], lags[0])
        product = narrow(wide_dot(jnp.concatenate(rows, axis=0), weight[0]))
        acc = [product[i * planes : (i + 1) * planes] for i in range(step)]
        for band in range(1, bands):
            rows = []
            patterns = []
            for orient in range(orients):
                pairs = [
                    harmonic_of(
                        table_ref[2 * orient, pl.ds(begin + i + shift, 1), :],
                        table_ref[2 * orient + 1, pl.ds(begin + i + shift, 1), :],
                        band,
                    )
                    for i in range(step + 2 * span)
                ]
                for part in range(2):
                    columns = [
                        pairs[i][part] * axial_ref[band, begin + i]
                        for i in range(step + 2 * span)
                    ]
                    rows += filtered(columns, lags[band])
                    patterns.append([pairs[i + span][part] for i in range(step)])
            product = narrow(wide_dot(jnp.concatenate(rows, axis=0), weight[band]))
            for which, pattern in enumerate(patterns):
                for i in range(step):
                    at = (which * step + i) * planes
                    acc[i] = acc[i] + pattern[i] * product[at : at + planes]
        for i in range(step):
            out_ref[begin + i] = acc[i]
        return carry

    lax.fori_loop(0, out_ref.shape[0] // step, chunk, 0)


def estimate_part(axial, table, row_blur, column_taps):
    _, extended, planes, row_count = axial.shape
    width = extended - 2 * (column_taps.shape[1] - 1)
    near = (table.shape[0], width + 2 * PAD, row_count)
    if width % 8:
        table = lax.dynamic_slice_in_dim(table, lax.axis_index("gz") * width, near[1], axis=1)
    smem = pl.BlockSpec(memory_space=pltpu.SMEM)
    vmem = pl.BlockSpec(memory_space=pltpu.VMEM)
    anywhere = pl.BlockSpec(memory_space=pltpu.HBM)
    rows = table.shape[0] * width * planes
    return pl.pallas_call(
        estimate_kernel,
        out_shape=jax.ShapeDtypeStruct((width, planes, row_count), jnp.float32),
        in_specs=[smem, vmem, anywhere, vmem],
        out_specs=vmem,
        scratch_shapes=[pltpu.VMEM(near, jnp.float32), pltpu.SemaphoreType.DMA],
        cost_estimate=pl.CostEstimate(
            flops=40 * rows * 2 * 256 * 256, bytes_accessed=axial.size * 4, transcendentals=0
        ),
        compiler_params=pltpu.CompilerParams(vmem_limit_bytes=40 << 20),
        name="estimate_part",
    )(column_taps, axial, table, row_blur)


def combine_kernel(adjoint_ref, estimate_ref, received_ref, out_ref):
    width, planes, row_count = estimate_ref.shape
    depth = adjoint_ref.shape[1]
    high, low = split(adjoint_ref[...])
    left_side = jnp.concatenate([high, high, low], axis=1)
    for index in range(0, width, 2):
        columns = [received_ref[pl.ds(index + i, depth, stride=width), :] for i in range(2)]
        high, low = split(jnp.concatenate(columns, axis=1))
        right_side = jnp.concatenate([high, low, high], axis=0)
        product = wide_dot(left_side, right_side)
        for i in range(2):
            out_ref[pl.ds(index + i, planes, stride=width), :] = (
                estimate_ref[index + i] - product[:, i * row_count : (i + 1) * row_count]
            )


def combine(forward, from_estimate, received):
    width, planes, row_count = from_estimate.shape
    depth = forward.shape[0] * planes
    adjoint = forward.transpose(2, 1, 0).reshape(planes, depth)
    vmem = pl.BlockSpec(memory_space=pltpu.VMEM)
    return pl.pallas_call(
        combine_kernel,
        out_shape=jax.ShapeDtypeStruct((planes * width, row_count), jnp.float32),
        in_specs=[vmem] * 3,
        out_specs=vmem,
        cost_estimate=pl.CostEstimate(
            flops=2 * received.size * planes, bytes_accessed=received.size * 4, transcendentals=0
        ),
        compiler_params=pltpu.CompilerParams(vmem_limit_bytes=24 << 20),
        name="combine",
    )(adjoint, from_estimate, received.reshape(depth * width, row_count)).reshape(
        planes, width, row_count
    )


def halo(estimate, span):
    ring = lax.axis_size("gz")
    width = estimate.shape[1]
    lefts, rights = [], []
    hop, missing = 1, span
    while missing > 0:
        take = min(missing, width)
        forth = [(s, (s + hop) % ring) for s in range(ring)]
        back = [(s, (s - hop) % ring) for s in range(ring)]
        lefts.insert(0, lax.ppermute(estimate[:, width - take :], "gz", forth))
        rights.append(lax.ppermute(estimate[:, :take], "gz", back))
        missing -= take
        hop += 1
    return lefts + [estimate] + rights


def axial_matrices(axial_otf, order):
    planes = order.shape[0]
    wrapped = np.arange(planes)[:, None] * np.arange(planes)[None, :] % planes
    angle = wrapped * (2.0 * math.pi / planes)
    cosine = np.cos(angle).astype(np.float32)
    sine = np.sin(angle).astype(np.float32)
    wrapped = order[:, None] * np.arange(planes, dtype=np.int32)[None, :] % planes
    angle = wrapped.astype(jnp.float32) * (2.0 * math.pi / planes)
    real = axial_otf[:, 0, :, None]
    imag = axial_otf[:, 1, :, None]
    inner = jnp.concatenate(
        [real * cosine + imag * sine, real * sine - imag * cosine], axis=1
    )
    both = jnp.concatenate([jnp.cos(angle), jnp.sin(angle)], axis=1) * (1.0 / planes)
    return jnp.einsum(
        "zk,mkw->mzw", both, inner, precision=lax.Precision.HIGHEST,
        preferred_element_type=jnp.float32,
    )


def by_permutes(ring):
    return ring <= 16 and ring & (ring - 1) == 0 and ring > 4


def exchange(sums):
    ring = lax.axis_size("gz")
    if len(sums) == 1:
        return lax.all_to_all(sums[0], "gz", 0, 0, tiled=True)
    chip = lax.axis_index("gz") // 2
    mine, other = sums
    other = lax.ppermute(other, "gz", [(s, s ^ 1) for s in range(ring)])
    both = jnp.stack([mine, other], axis=1)
    parts = []
    for bit in range(ring // 2):
        part = lax.dynamic_index_in_dim(both, chip ^ bit, 0, keepdims=False)
        if bit:
            part = lax.ppermute(part, "gz", [(s, s ^ (2 * bit)) for s in range(ring)])
        parts.append(part)
    return jnp.concatenate(parts, axis=0)


def shards(estimate, frames, phase_index, axial_otf, row_blur, column_taps):
    planes, width, row_count = estimate.shape
    ring = lax.axis_size("gz")
    orients = frames.shape[0]
    bands = row_blur.shape[0]
    span = column_taps.shape[1] - 1
    table = jnp.asarray(pattern_table(orients, width * ring, row_count, PAD))
    cores = 2 if by_permutes(ring) else 1
    sums = data_sums(frames, phase_index, row_blur, column_taps, table, ring, cores)
    estimate, *sums = lax.optimization_barrier((estimate, *sums))
    pieces = halo(estimate, span)
    received = exchange(sums)
    order = jnp.arange(planes, dtype=jnp.int32)
    if by_permutes(ring):
        order = order ^ lax.axis_index("gz")
    forward = axial_matrices(axial_otf, order)
    squared = jnp.einsum("mzw,mzv->mwv", forward, forward, precision=lax.Precision.HIGHEST)
    extended = jnp.concatenate(pieces, axis=1)
    axial = exact_dot(squared.reshape(bands * planes, planes), extended.reshape(planes, -1))
    axial = axial.reshape(bands, planes, width + 2 * span, row_count)
    axial = axial.transpose(0, 2, 1, 3)
    from_estimate = estimate_part(axial, table, row_blur, column_taps)
    return combine(forward, from_estimate, received)


def solution(mesh):
    placed = (P(None, "gz", "groups"), P(None, None, "gz", None, "groups"), P(), P(), P(), P())
    return jax.shard_map(
        shards, mesh=mesh, in_specs=placed, out_specs=P(None, "gz", "groups"), check_vma=False
    )
```

profile of v0, /device:TPU:0, one launch (start us, length us, event | category | flops | bytes accessed | tf_op | source)
XLA Modules:
  0.0 44.3 jit_solution(3137633149836327292)
XLA Ops:
  0.0 0.0 copy-start.5
  0.0 0.0 copy-start.6
  0.0 0.0 copy-start.4
  0.0 0.0 copy-start.7
  0.0 6.4 %data_sums.1 = (f32[8,3,32,128]{3,2,1,0:T(8,128)}, f32[8,3,32,128]{3,2,1,0:T(8,128)}) custom-call(s32[3,5]{1,0:T(4,128)} %phase_hbm.1, f32[3,7]{1,0:T(4,128)} %taps_ref.1, s32[3,5,1,512,128]{4,3,2,1,0:T(8,128)} %frames_hbm.1, f32[3,128,128]{2,1,0:T(8,128)} %blur_ref.1, f32[6,528,128]{2,1,0:T(8,128)} %constant.75.clone.table_hbm), custom_call_target="tpu_custom_call" | custom-call | flops 872415232 | bytes 3932160 | tf_op jit(solution)/shard_map/data_sums/pallas_call | solution.py:242
  6.4 0.0 copy-start
  6.4 0.0 copy-start.1
  6.5 0.0 copy-start.2
  6.5 0.0 copy-done.4
  6.5 0.6 %collective-permute-start = (f32[16,6,128]{2,1,0:T(8,128)S(1)}, f32[16,6,128]{2,1,0:T(8,128)S(1)}, u32[]{:S(2)}, u32[]{:S(2)}) collective-permute-start(f32[16,6,128]{2,1,0:T(8,128)S(1)} %get-tuple-element.21), channel_id=1, source_target_pairs={{0,1},{1,2},{2,3},{3,4},{4,5},{5,6},{6,7},{7,8},{8,9},{9,10},{10,1... | collective-permute-start | bytes 147464 | tf_op jit(solution)/shard_map/ppermute | solution.py:427
  7.1 5.0 %collective-permute-start.1 = (f32[16,6,128]{2,1,0:T(8,128)S(1)}, f32[16,6,128]{2,1,0:T(8,128)S(1)}, u32[]{:S(2)}, u32[]{:S(2)}) collective-permute-start(f32[16,6,128]{2,1,0:T(8,128)S(1)} %get-tuple-element.22), channel_id=1, source_target_pairs={{0,15},{1,0},{2,1},{3,2},{4,3},{5,4},{6,5},{7,6},{8,7},{9,8},{10,9... | collective-permute-start | bytes 147464 | tf_op jit(solution)/shard_map/ppermute | solution.py:428
  12.1 0.0 collective-permute-start.2
  12.1 0.0 copy-done.7
  12.1 0.1 fusion.34
  12.3 0.0 copy-done.5
  12.3 0.0 copy-done.6
  12.3 0.2 fusion.18
  12.5 0.2 convolution_bitcast_fusion.1
  12.8 0.1 copy.12
  12.9 0.1 copy.14.adjoint_ref
  12.9 1.2 %collective-permute-done = f32[16,6,128]{2,1,0:T(8,128)S(1)} collective-permute-done((f32[16,6,128]{2,1,0:T(8,128)S(1)}, f32[16,6,128]{2,1,0:T(8,128)S(1)}, u32[]{:S(2)}, u32[]{:S(2)}) %collective-permute-start) | collective-permute-done | bytes 49184 | tf_op jit(solution)/shard_map/ppermute | solution.py:427
  14.1 0.0 collective-permute-done.1
  14.1 1.0 %convolution_bitcast_fusion.axial_ref = f32[3,44,16,128]{3,2,1,0:T(8,128)S(1)} fusion(f32[3,16,16,1]{2,1,3,0:T(8,128)S(1)} %convolution_bitcast_fusion.1, f32[2,8,44,128]{3,2,1,0:T(8,128)S(1)} %bitcast.64), kind=kOutput, calls=%fused_computation.16 | convolution fusion | flops 51904512 | bytes 1444864 | tf_op jit(solution)/shard_map/dot_general | solution.py:19
  15.1 0.0 copy-done
  15.1 0.0 copy-done.1
  15.2 0.0 copy-done.2
  15.2 0.0 copy-start.3
  15.2 4.6 %estimate_part.1.estimate_ref = f32[32,16,128]{2,1,0:T(8,128)S(1)} custom-call(f32[3,7]{1,0:T(4,128)S(1)} %copy-done.2, f32[3,44,16,128]{3,2,1,0:T(8,128)S(1)} %convolution_bitcast_fusion.axial_ref, f32[6,528,128]{2,1,0:T(8,128)S(1)} %copy-done, f32[3,128,128]{2,1,0:T(8,128)S(1)} %copy-done.1), custom_call_target="tpu_custom_call" | custom-call | flops 16106127360 | bytes 1081344 | tf_op jit(solution)/shard_map/estimate_part/pallas_call | solution.py:368
  19.8 0.0 collective-permute-done.2
  19.8 0.0 copy-done.3
  19.9 2.2 %collective-permute-start.8 = (f32[2,3,32,128]{3,2,1,0:T(8,128)S(1)}, f32[2,3,32,128]{3,2,1,0:T(8,128)S(1)}, u32[]{:S(2)}, u32[]{:S(2)}) collective-permute-start(f32[2,3,32,128]{3,2,1,0:T(8,128)S(1)} %fusion.17), channel_id=1, source_target_pairs={{0,12},{1,13},{2,14},{3,15},{4,8},{5,9},{6,10},{7,11},{8,4},{9,5},... | collective-permute-start | bytes 294920 | tf_op jit(solution)/shard_map/ppermute | solution.py:470
  22.1 0.3 collective-permute-start.9
  22.5 2.9 %collective-permute-start.3 = (f32[2,3,32,128]{3,2,1,0:T(8,128)S(1)}, f32[2,3,32,128]{3,2,1,0:T(8,128)S(1)}, u32[]{:S(2)}, u32[]{:S(2)}) collective-permute-start(f32[2,3,32,128]{3,2,1,0:T(8,128)S(1)} %get-tuple-element.16), channel_id=1, source_target_pairs={{0,2},{1,3},{2,0},{3,1},{4,6},{5,7},{6,4},{7,5},{8,10},{9,11},{10,... | collective-permute-start | bytes 294920 | tf_op jit(solution)/shard_map/ppermute | solution.py:470
  25.3 0.0 collective-permute-start.4
  25.3 1.5 %collective-permute-start.5 = (f32[2,3,32,128]{3,2,1,0:T(8,128)S(1)}, f32[2,3,32,128]{3,2,1,0:T(8,128)S(1)}, u32[]{:S(2)}, u32[]{:S(2)}) collective-permute-start(f32[2,3,32,128]{3,2,1,0:T(8,128)S(1)} %get-tuple-element.18), channel_id=1, source_target_pairs={{0,6},{1,7},{2,4},{3,5},{4,2},{5,3},{6,0},{7,1},{8,14},{9,15},{10,... | collective-permute-start | bytes 294920 | tf_op jit(solution)/shard_map/ppermute | solution.py:470
  26.8 4.0 %collective-permute-done.3 = f32[2,3,32,128]{3,2,1,0:T(8,128)S(1)} collective-permute-done((f32[2,3,32,128]{3,2,1,0:T(8,128)S(1)}, f32[2,3,32,128]{3,2,1,0:T(8,128)S(1)}, u32[]{:S(2)}, u32[]{:S(2)}) %collective-permute-start.3) | collective-permute-done | bytes 98336 | tf_op jit(solution)/shard_map/ppermute | solution.py:470
  30.8 0.0 collective-permute-start.6
  30.8 1.3 %collective-permute-done.4 = f32[2,3,32,128]{3,2,1,0:T(8,128)S(1)} collective-permute-done((f32[2,3,32,128]{3,2,1,0:T(8,128)S(1)}, f32[2,3,32,128]{3,2,1,0:T(8,128)S(1)}, u32[]{:S(2)}, u32[]{:S(2)}) %collective-permute-start.4) | collective-permute-done | bytes 98336 | tf_op jit(solution)/shard_map/ppermute | solution.py:470
  32.0 2.1 %collective-permute-start.7 = (f32[2,3,32,128]{3,2,1,0:T(8,128)S(1)}, f32[2,3,32,128]{3,2,1,0:T(8,128)S(1)}, u32[]{:S(2)}, u32[]{:S(2)}) collective-permute-start(f32[2,3,32,128]{3,2,1,0:T(8,128)S(1)} %get-tuple-element.20), channel_id=1, source_target_pairs={{0,10},{1,11},{2,8},{3,9},{4,14},{5,15},{6,12},{7,13},{8,2},{9,3},... | collective-permute-start | bytes 294920 | tf_op jit(solution)/shard_map/ppermute | solution.py:470
  34.1 1.3 %collective-permute-done.5 = f32[2,3,32,128]{3,2,1,0:T(8,128)S(1)} collective-permute-done((f32[2,3,32,128]{3,2,1,0:T(8,128)S(1)}, f32[2,3,32,128]{3,2,1,0:T(8,128)S(1)}, u32[]{:S(2)}, u32[]{:S(2)}) %collective-permute-start.5) | collective-permute-done | bytes 98336 | tf_op jit(solution)/shard_map/ppermute | solution.py:470
  35.4 5.6 %collective-permute-done.6 = f32[2,3,32,128]{3,2,1,0:T(8,128)S(1)} collective-permute-done((f32[2,3,32,128]{3,2,1,0:T(8,128)S(1)}, f32[2,3,32,128]{3,2,1,0:T(8,128)S(1)}, u32[]{:S(2)}, u32[]{:S(2)}) %collective-permute-start.6) | collective-permute-done | bytes 98336 | tf_op jit(solution)/shard_map/ppermute | solution.py:470
  41.0 1.9 %collective-permute-done.7 = f32[2,3,32,128]{3,2,1,0:T(8,128)S(1)} collective-permute-done((f32[2,3,32,128]{3,2,1,0:T(8,128)S(1)}, f32[2,3,32,128]{3,2,1,0:T(8,128)S(1)}, u32[]{:S(2)}, u32[]{:S(2)}) %collective-permute-start.7) | collective-permute-done | bytes 98336 | tf_op jit(solution)/shard_map/ppermute | solution.py:470
  42.9 0.0 collective-permute-done.8
  42.9 0.0 collective-permute-done.9
  42.9 1.3 %combine.1 = f32[512,128]{1,0:T(8,128)} custom-call(f32[16,48]{1,0:T(8,128)S(1)} %copy.14.adjoint_ref, f32[32,16,128]{2,1,0:T(8,128)S(1)} %estimate_part.1.estimate_ref, f32[1536,128]{1,0:T(8,128)S(1)} %bitcast.57), custom_call_target="tpu_custom_call" | custom-call | flops 6291456 | bytes 786432 | tf_op jit(solution)/shard_map/combine/pallas_call | solution.py:403
  (17 shorter events, 0.2 us)
Async XLA Ops:
  0.0 12.3 %copy-start.5 = (f32[16,16]{0,1:T(8,128)S(1)}, f32[16,16]{0,1:T(8,128)}, u32[]{:S(2)}) copy-start(f32[16,16]{0,1:T(8,128)} %constant.78.clone) | copy-start | bytes 3076
  0.0 12.3 %copy-start.6 = (f32[16,16]{0,1:T(8,128)S(1)}, f32[16,16]{0,1:T(8,128)}, u32[]{:S(2)}) copy-start(f32[16,16]{0,1:T(8,128)} %constant.77.clone) | copy-start | bytes 3076
  0.0 6.5 %copy-start.4 = (f32[16,32,128]{2,1,0:T(8,128)S(1)}, f32[16,32,128]{2,1,0:T(8,128)}, u32[]{:S(2)}) copy-start(f32[16,32,128]{2,1,0:T(8,128)} %param.10) | copy-start | bytes 786436
  0.0 12.1 %copy-start.7 = (f32[3,2,16]{2,1,0:T(2,128)S(1)}, f32[3,2,16]{2,1,0:T(2,128)}, u32[]{:S(2)}) copy-start(f32[3,2,16]{2,1,0:T(2,128)} %param.13) | copy-start | bytes 1156
  6.4 8.7 %copy-start = (f32[6,528,128]{2,1,0:T(8,128)S(1)}, f32[6,528,128]{2,1,0:T(8,128)}, u32[]{:S(2)}) copy-start(f32[6,528,128]{2,1,0:T(8,128)} %constant.75.clone.table_hbm) | copy-start | bytes 4866052
  6.4 8.7 %copy-start.1 = (f32[3,128,128]{2,1,0:T(8,128)S(1)}, f32[3,128,128]{2,1,0:T(8,128)}, u32[]{:S(2)}) copy-start(f32[3,128,128]{2,1,0:T(8,128)} %blur_ref.1) | copy-start | bytes 589828
  6.5 8.7 %copy-start.2 = (f32[3,7]{1,0:T(4,128)S(1)}, f32[3,7]{1,0:T(4,128)}, u32[]{:S(2)}) copy-start(f32[3,7]{1,0:T(4,128)} %taps_ref.1) | copy-start | bytes 256
  6.5 7.6 %collective-permute-start = (f32[16,6,128]{2,1,0:T(8,128)S(1)}, f32[16,6,128]{2,1,0:T(8,128)S(1)}, u32[]{:S(2)}, u32[]{:S(2)}) collective-permute-start(f32[16,6,128]{2,1,0:T(8,128)S(1)} %get-tuple-element.21), channel_id=1, source_target_pairs={{0,1},{1,2},{2,3},{3,4},{4,5},{5,6},{6,7},{7,8},{8,9},{9,10},{10,1... | collective-permute-start | bytes 147464 | tf_op jit(solution)/shard_map/ppermute | solution.py:427
  7.1 7.0 %collective-permute-start.1 = (f32[16,6,128]{2,1,0:T(8,128)S(1)}, f32[16,6,128]{2,1,0:T(8,128)S(1)}, u32[]{:S(2)}, u32[]{:S(2)}) collective-permute-start(f32[16,6,128]{2,1,0:T(8,128)S(1)} %get-tuple-element.22), channel_id=1, source_target_pairs={{0,15},{1,0},{2,1},{3,2},{4,3},{5,4},{6,5},{7,6},{8,7},{9,8},{10,9... | collective-permute-start | bytes 147464 | tf_op jit(solution)/shard_map/ppermute | solution.py:428
  12.1 7.7 %collective-permute-start.2 = (f32[8,3,32,128]{3,2,1,0:T(8,128)}, f32[8,3,32,128]{3,2,1,0:T(8,128)S(1)}, u32[]{:S(2)}, u32[]{:S(2)}) collective-permute-start(f32[8,3,32,128]{3,2,1,0:T(8,128)} %get-tuple-element.14), channel_id=1, source_target_pairs={{0,1},{1,0},{2,3},{3,2},{4,5},{5,4},{6,7},{7,6},{8,9},{9,8},{10,11... | collective-permute-start | bytes 1179656 | tf_op jit(solution)/shard_map/ppermute | solution.py:464
  15.2 4.7 %copy-start.3 = (f32[8,3,32,128]{3,2,1,0:T(8,128)S(1)}, f32[8,3,32,128]{3,2,1,0:T(8,128)}, u32[]{:S(2)}) copy-start(f32[8,3,32,128]{3,2,1,0:T(8,128)} %get-tuple-element.13) | copy-start | bytes 1179652
  19.9 23.0 %collective-permute-start.8 = (f32[2,3,32,128]{3,2,1,0:T(8,128)S(1)}, f32[2,3,32,128]{3,2,1,0:T(8,128)S(1)}, u32[]{:S(2)}, u32[]{:S(2)}) collective-permute-start(f32[2,3,32,128]{3,2,1,0:T(8,128)S(1)} %fusion.17), channel_id=1, source_target_pairs={{0,12},{1,13},{2,14},{3,15},{4,8},{5,9},{6,10},{7,11},{8,4},{9,5},... | collective-permute-start | bytes 294920 | tf_op jit(solution)/shard_map/ppermute | solution.py:470
  22.1 20.8 %collective-permute-start.9 = (f32[2,3,32,128]{3,2,1,0:T(8,128)S(1)}, f32[2,3,32,128]{3,2,1,0:T(8,128)S(1)}, u32[]{:S(2)}, u32[]{:S(2)}) collective-permute-start(f32[2,3,32,128]{3,2,1,0:T(8,128)S(1)} %get-tuple-element.15), channel_id=1, source_target_pairs={{0,14},{1,15},{2,12},{3,13},{4,10},{5,11},{6,8},{7,9},{8,6},{9,7},... | collective-permute-start | bytes 294920 | tf_op jit(solution)/shard_map/ppermute | solution.py:470
  22.5 8.3 %collective-permute-start.3 = (f32[2,3,32,128]{3,2,1,0:T(8,128)S(1)}, f32[2,3,32,128]{3,2,1,0:T(8,128)S(1)}, u32[]{:S(2)}, u32[]{:S(2)}) collective-permute-start(f32[2,3,32,128]{3,2,1,0:T(8,128)S(1)} %get-tuple-element.16), channel_id=1, source_target_pairs={{0,2},{1,3},{2,0},{3,1},{4,6},{5,7},{6,4},{7,5},{8,10},{9,11},{10,... | collective-permute-start | bytes 294920 | tf_op jit(solution)/shard_map/ppermute | solution.py:470
  25.3 6.7 %collective-permute-start.4 = (f32[2,3,32,128]{3,2,1,0:T(8,128)S(1)}, f32[2,3,32,128]{3,2,1,0:T(8,128)S(1)}, u32[]{:S(2)}, u32[]{:S(2)}) collective-permute-start(f32[2,3,32,128]{3,2,1,0:T(8,128)S(1)} %get-tuple-element.17), channel_id=1, source_target_pairs={{0,4},{1,5},{2,6},{3,7},{4,0},{5,1},{6,2},{7,3},{8,12},{9,13},{10,... | collective-permute-start | bytes 294920 | tf_op jit(solution)/shard_map/ppermute | solution.py:470
  25.3 10.1 %collective-permute-start.5 = (f32[2,3,32,128]{3,2,1,0:T(8,128)S(1)}, f32[2,3,32,128]{3,2,1,0:T(8,128)S(1)}, u32[]{:S(2)}, u32[]{:S(2)}) collective-permute-start(f32[2,3,32,128]{3,2,1,0:T(8,128)S(1)} %get-tuple-element.18), channel_id=1, source_target_pairs={{0,6},{1,7},{2,4},{3,5},{4,2},{5,3},{6,0},{7,1},{8,14},{9,15},{10,... | collective-permute-start | bytes 294920 | tf_op jit(solution)/shard_map/ppermute | solution.py:470
  30.8 10.2 %collective-permute-start.6 = (f32[2,3,32,128]{3,2,1,0:T(8,128)S(1)}, f32[2,3,32,128]{3,2,1,0:T(8,128)S(1)}, u32[]{:S(2)}, u32[]{:S(2)}) collective-permute-start(f32[2,3,32,128]{3,2,1,0:T(8,128)S(1)} %get-tuple-element.19), channel_id=1, source_target_pairs={{0,8},{1,9},{2,10},{3,11},{4,12},{5,13},{6,14},{7,15},{8,0},{9,1},... | collective-permute-start | bytes 294920 | tf_op jit(solution)/shard_map/ppermute | solution.py:470
  32.0 10.8 %collective-permute-start.7 = (f32[2,3,32,128]{3,2,1,0:T(8,128)S(1)}, f32[2,3,32,128]{3,2,1,0:T(8,128)S(1)}, u32[]{:S(2)}, u32[]{:S(2)}) collective-permute-start(f32[2,3,32,128]{3,2,1,0:T(8,128)S(1)} %get-tuple-element.20), channel_id=1, source_target_pairs={{0,10},{1,11},{2,8},{3,9},{4,14},{5,15},{6,12},{7,13},{8,2},{9,3},... | collective-permute-start | bytes 294920 | tf_op jit(solution)/shard_map/ppermute | solution.py:470
where the time goes:
time: 44.4 us; the launch traced here: 44.3 us
  waiting for transfers between devices  15.1 us (34%)
  starting transfers between devices  14.5 us (33%)
  Pallas kernels  12.4 us (28%)
  matrix products  1.37 us (3%)
    ppermute x7, waiting for transfers between devices, exchange(): part = lax.ppermute(part, 'gz', [(s, s ^ 2 * bit) for s in range(ring)])  14 us
    ppermute x7, starting transfers between devices, exchange(): part = lax.ppermute(part, 'gz', [(s, s ^ 2 * bit) for s in range(ring)])  8.94 us
    pallas_call x1, Pallas kernels, data_sums(): pl.pallas_call(data_kernel, out_shape=[jax.ShapeDtypeStruct((chunks // co...  6.41 us
    ppermute x1, starting transfers between devices, halo(): rights.append(lax.ppermute(estimate[:, :take], 'gz', back))  5.05 us
    pallas_call x1, Pallas kernels, estimate_part(): pl.pallas_call(estimate_kernel, out_shape=jax.ShapeDtypeStruct((width, pl...  4.64 us
    pallas_call x1, Pallas kernels, combine(): pl.pallas_call(combine_kernel, out_shape=jax.ShapeDtypeStruct((planes * w...  1.32 us
    ppermute x1, waiting for transfers between devices, halo(): lefts.insert(0, lax.ppermute(estimate[:, width - take:], 'gz', forth))  1.17 us
    dot_general x1, matrix products, exact_dot(): jnp.dot(left_side, right_side, preferred_element_type=jnp.float32, precis...  0.99 us
  transfers between devices with their start and end apart: 10, of which 6 were waited for; matrix products, arithmetic and copies ran while one was open for 4% of the time, Pallas kernels for 10%

commit v1 on v0

--- a/solution.py
+++ b/solution.py
@@ -391,7 +391,7 @@
         product = wide_dot(left_side, right_side)
         for i in range(2):
             out_ref[pl.ds(index + i, planes, stride=width), :] = (
-                estimate_ref[index + i] - product[:, i * row_count : (i + 1) * row_count]
+                estimate_ref[index + i] + product[:, i * row_count : (i + 1) * row_count]
             )
 
 
@@ -458,11 +458,12 @@
 def exchange(sums):
     ring = lax.axis_size("gz")
     if len(sums) == 1:
-        return lax.all_to_all(sums[0], "gz", 0, 0, tiled=True)
+        return lax.all_to_all(-sums[0], "gz", 0, 0, tiled=True)
     chip = lax.axis_index("gz") // 2
     mine, other = sums
     other = lax.ppermute(other, "gz", [(s, s ^ 1) for s in range(ring)])
-    both = jnp.stack([mine, other], axis=1)
+    mine = lax.optimization_barrier(-mine)
+    both = jnp.stack([mine, -other], axis=1)
     parts = []
     for bit in range(ring // 2):
         part = lax.dynamic_index_in_dim(both, chip ^ bit, 0, keepdims=False)

time: 44.4 us -> 44.3 us (level)
  waiting for transfers between devices: 15.1 us -> 13.6 us
  other arithmetic: 0.25 us -> 1.43 us
    ppermute x1, waiting for transfers between devices: 1.17 us -> 0.01 us  [halo(): lefts.insert(0, lax.ppermute(estimate[:, width - take:], 'gz', forth))]
    neg x0 -> x1, other arithmetic: none -> 1.15 us  [exchange(): mine = lax.optimization_barrier(-mine)]
  transfers between devices with their start and end apart: 10 -> 10, of which waited for: 6 -> 5; matrix products, arithmetic and copies ran while one was open for 4% -> 7% of each run, Pallas kernels for 10% -> 10%
where the time goes in v1:
time: 44.3 us; the launch traced here: 44.1 us
  starting transfers between devices  14.8 us (33%)
  waiting for transfers between devices  13.6 us (31%)
  Pallas kernels  12.3 us (28%)
  other arithmetic  1.43 us (3%)
  matrix products  1.37 us (3%)
    ppermute x7, waiting for transfers between devices, exchange(): part = lax.ppermute(part, 'gz', [(s, s ^ 2 * bit) for s in range(ring)])  13.6 us
    ppermute x7, starting transfers between devices, exchange(): part = lax.ppermute(part, 'gz', [(s, s ^ 2 * bit) for s in range(ring)])  9.23 us
    pallas_call x1, Pallas kernels, data_sums(): pl.pallas_call(data_kernel, out_shape=[jax.ShapeDtypeStruct((chunks // co...  6.4 us
    ppermute x1, starting transfers between devices, halo(): rights.append(lax.ppermute(estimate[:, :take], 'gz', back))  5.05 us
    pallas_call x1, Pallas kernels, estimate_part(): pl.pallas_call(estimate_kernel, out_shape=jax.ShapeDtypeStruct((width, pl...  4.54 us
    pallas_call x1, Pallas kernels, combine(): pl.pallas_call(combine_kernel, out_shape=jax.ShapeDtypeStruct((planes * w...  1.32 us
    neg x1, other arithmetic, exchange(): mine = lax.optimization_barrier(-mine)  1.15 us
    dot_general x1, matrix products, exact_dot(): jnp.dot(left_side, right_side, preferred_element_type=jnp.float32, precis...  0.99 us
  transfers between devices with their start and end apart: 10, of which 5 were waited for; matrix products, arithmetic and copies ran while one was open for 7% of the time, Pallas kernels for 10%

profile of v1, /device:TPU:0, one launch (start us, length us, event | category | flops | bytes accessed | tf_op | source)
XLA Modules:
  0.0 44.1 jit_solution(6854809352971545366)
XLA Ops:
  0.0 0.0 copy-start.4
  0.0 0.0 copy-start.5
  0.0 0.0 copy-start.3
  0.0 0.0 copy-start.6
  0.0 6.4 %data_sums.1 = (f32[8,3,32,128]{3,2,1,0:T(8,128)}, f32[8,3,32,128]{3,2,1,0:T(8,128)}) custom-call(s32[3,5]{1,0:T(4,128)} %phase_hbm.1, f32[3,7]{1,0:T(4,128)} %taps_ref.1, s32[3,5,1,512,128]{4,3,2,1,0:T(8,128)} %frames_hbm.1, f32[3,128,128]{2,1,0:T(8,128)} %blur_ref.1, f32[6,528,128]{2,1,0:T(8,128)} %constant.75.clone.table_hbm), custom_call_target="tpu_custom_call" | custom-call | flops 872415232 | bytes 3932160 | tf_op jit(solution)/shard_map/data_sums/pallas_call | solution.py:242
  6.4 0.0 copy-done.3
  6.4 0.6 %collective-permute-start = (f32[16,6,128]{2,1,0:T(8,128)S(1)}, f32[16,6,128]{2,1,0:T(8,128)S(1)}, u32[]{:S(2)}, u32[]{:S(2)}) collective-permute-start(f32[16,6,128]{2,1,0:T(8,128)S(1)} %get-tuple-element.21), channel_id=1, source_target_pairs={{0,1},{1,2},{2,3},{3,4},{4,5},{5,6},{6,7},{7,8},{8,9},{9,10},{10,1... | collective-permute-start | bytes 147464 | tf_op jit(solution)/shard_map/ppermute | solution.py:427
  7.0 5.0 %collective-permute-start.1 = (f32[16,6,128]{2,1,0:T(8,128)S(1)}, f32[16,6,128]{2,1,0:T(8,128)S(1)}, u32[]{:S(2)}, u32[]{:S(2)}) collective-permute-start(f32[16,6,128]{2,1,0:T(8,128)S(1)} %get-tuple-element.22), channel_id=1, source_target_pairs={{0,15},{1,0},{2,1},{3,2},{4,3},{5,4},{6,5},{7,6},{8,7},{9,8},{10,9... | collective-permute-start | bytes 147464 | tf_op jit(solution)/shard_map/ppermute | solution.py:428
  12.1 0.0 collective-permute-start.2
  12.1 0.0 copy-done.6
  12.1 0.1 fusion.34
  12.2 0.0 copy-done.4
  12.2 0.0 copy-done.5
  12.3 0.2 fusion.18
  12.5 0.2 convolution_bitcast_fusion.1
  12.7 0.0 copy-start
  12.7 0.0 copy-start.1
  12.7 0.0 copy-start.2
  12.7 0.1 copy.12
  12.8 0.1 copy.14.adjoint_ref
  12.9 1.1 %neg.6 = f32[8,3,32,128]{3,2,1,0:T(8,128)S(1)} negate(f32[8,3,32,128]{3,2,1,0:T(8,128)} %get-tuple-element.13) | non-fusion elementwise | flops 98304 | bytes 786432 | tf_op jit(solution)/shard_map/neg | solution.py:465
  14.1 0.0 collective-permute-done
  14.1 0.0 collective-permute-done.1
  14.2 1.0 %convolution_bitcast_fusion.axial_ref = f32[3,44,16,128]{3,2,1,0:T(8,128)S(1)} fusion(f32[3,16,16,1]{2,1,3,0:T(8,128)S(1)} %convolution_bitcast_fusion.1, f32[2,8,44,128]{3,2,1,0:T(8,128)S(1)} %bitcast.62), kind=kOutput, calls=%fused_computation.16 | convolution fusion | flops 51904512 | bytes 1444864 | tf_op jit(solution)/shard_map/dot_general | solution.py:19
  15.2 0.0 copy-done
  15.2 0.0 copy-done.1
  15.2 0.0 copy-done.2
  15.2 4.5 %estimate_part.1.estimate_ref = f32[32,16,128]{2,1,0:T(8,128)S(1)} custom-call(f32[3,7]{1,0:T(4,128)S(1)} %copy-done.2, f32[3,44,16,128]{3,2,1,0:T(8,128)S(1)} %convolution_bitcast_fusion.axial_ref, f32[6,528,128]{2,1,0:T(8,128)S(1)} %copy-done, f32[3,128,128]{2,1,0:T(8,128)S(1)} %copy-done.1), custom_call_target="tpu_custom_call" | custom-call | flops 16106127360 | bytes 1081344 | tf_op jit(solution)/shard_map/estimate_part/pallas_call | solution.py:368
  19.8 0.0 collective-permute-done.2
  19.8 2.3 %collective-permute-start.8 = (f32[2,3,32,128]{3,2,1,0:T(8,128)S(1)}, f32[2,3,32,128]{3,2,1,0:T(8,128)S(1)}, u32[]{:S(2)}, u32[]{:S(2)}) collective-permute-start(f32[2,3,32,128]{3,2,1,0:T(8,128)S(1)} %fusion.17), channel_id=1, source_target_pairs={{0,12},{1,13},{2,14},{3,15},{4,8},{5,9},{6,10},{7,11},{8,4},{9,5},... | collective-permute-start | bytes 294920 | tf_op jit(solution)/shard_map/ppermute | solution.py:471
  22.1 0.3 collective-permute-start.9
  22.5 2.8 %collective-permute-start.3 = (f32[2,3,32,128]{3,2,1,0:T(8,128)S(1)}, f32[2,3,32,128]{3,2,1,0:T(8,128)S(1)}, u32[]{:S(2)}, u32[]{:S(2)}) collective-permute-start(f32[2,3,32,128]{3,2,1,0:T(8,128)S(1)} %get-tuple-element.16), channel_id=1, source_target_pairs={{0,2},{1,3},{2,0},{3,1},{4,6},{5,7},{6,4},{7,5},{8,10},{9,11},{10,... | collective-permute-start | bytes 294920 | tf_op jit(solution)/shard_map/ppermute | solution.py:471
  25.3 0.0 collective-permute-start.4
  25.3 1.5 %collective-permute-start.5 = (f32[2,3,32,128]{3,2,1,0:T(8,128)S(1)}, f32[2,3,32,128]{3,2,1,0:T(8,128)S(1)}, u32[]{:S(2)}, u32[]{:S(2)}) collective-permute-start(f32[2,3,32,128]{3,2,1,0:T(8,128)S(1)} %get-tuple-element.18), channel_id=1, source_target_pairs={{0,6},{1,7},{2,4},{3,5},{4,2},{5,3},{6,0},{7,1},{8,14},{9,15},{10,... | collective-permute-start | bytes 294920 | tf_op jit(solution)/shard_map/ppermute | solution.py:471
  26.8 4.1 %collective-permute-done.3 = f32[2,3,32,128]{3,2,1,0:T(8,128)S(1)} collective-permute-done((f32[2,3,32,128]{3,2,1,0:T(8,128)S(1)}, f32[2,3,32,128]{3,2,1,0:T(8,128)S(1)}, u32[]{:S(2)}, u32[]{:S(2)}) %collective-permute-start.3) | collective-permute-done | bytes 98336 | tf_op jit(solution)/shard_map/ppermute | solution.py:471
  30.8 0.0 collective-permute-start.6
  30.8 1.1 %collective-permute-done.4 = f32[2,3,32,128]{3,2,1,0:T(8,128)S(1)} collective-permute-done((f32[2,3,32,128]{3,2,1,0:T(8,128)S(1)}, f32[2,3,32,128]{3,2,1,0:T(8,128)S(1)}, u32[]{:S(2)}, u32[]{:S(2)}) %collective-permute-start.4) | collective-permute-done | bytes 98336 | tf_op jit(solution)/shard_map/ppermute | solution.py:471
  32.0 2.3 %collective-permute-start.7 = (f32[2,3,32,128]{3,2,1,0:T(8,128)S(1)}, f32[2,3,32,128]{3,2,1,0:T(8,128)S(1)}, u32[]{:S(2)}, u32[]{:S(2)}) collective-permute-start(f32[2,3,32,128]{3,2,1,0:T(8,128)S(1)} %get-tuple-element.20), channel_id=1, source_target_pairs={{0,10},{1,11},{2,8},{3,9},{4,14},{5,15},{6,12},{7,13},{8,2},{9,3},... | collective-permute-start | bytes 294920 | tf_op jit(solution)/shard_map/ppermute | solution.py:471
  34.3 0.9 %collective-permute-done.5 = f32[2,3,32,128]{3,2,1,0:T(8,128)S(1)} collective-permute-done((f32[2,3,32,128]{3,2,1,0:T(8,128)S(1)}, f32[2,3,32,128]{3,2,1,0:T(8,128)S(1)}, u32[]{:S(2)}, u32[]{:S(2)}) %collective-permute-start.5) | collective-permute-done | bytes 98336 | tf_op jit(solution)/shard_map/ppermute | solution.py:471
  35.3 5.6 %collective-permute-done.6 = f32[2,3,32,128]{3,2,1,0:T(8,128)S(1)} collective-permute-done((f32[2,3,32,128]{3,2,1,0:T(8,128)S(1)}, f32[2,3,32,128]{3,2,1,0:T(8,128)S(1)}, u32[]{:S(2)}, u32[]{:S(2)}) %collective-permute-start.6) | collective-permute-done | bytes 98336 | tf_op jit(solution)/shard_map/ppermute | solution.py:471
  40.9 1.8 %collective-permute-done.7 = f32[2,3,32,128]{3,2,1,0:T(8,128)S(1)} collective-permute-done((f32[2,3,32,128]{3,2,1,0:T(8,128)S(1)}, f32[2,3,32,128]{3,2,1,0:T(8,128)S(1)}, u32[]{:S(2)}, u32[]{:S(2)}) %collective-permute-start.7) | collective-permute-done | bytes 98336 | tf_op jit(solution)/shard_map/ppermute | solution.py:471
  42.7 0.0 collective-permute-done.8
  42.8 0.0 collective-permute-done.9
  42.8 1.3 %combine.1 = f32[512,128]{1,0:T(8,128)} custom-call(f32[16,48]{1,0:T(8,128)S(1)} %copy.14.adjoint_ref, f32[32,16,128]{2,1,0:T(8,128)S(1)} %estimate_part.1.estimate_ref, f32[1536,128]{1,0:T(8,128)S(1)} %bitcast.58), custom_call_target="tpu_custom_call" | custom-call | flops 6291456 | bytes 786432 | tf_op jit(solution)/shard_map/combine/pallas_call | solution.py:403
  (18 shorter events, 0.3 us)
Async XLA Ops:
  0.0 12.2 %copy-start.4 = (f32[16,16]{0,1:T(8,128)S(1)}, f32[16,16]{0,1:T(8,128)}, u32[]{:S(2)}) copy-start(f32[16,16]{0,1:T(8,128)} %constant.78.clone) | copy-start | bytes 3076
  0.0 12.2 %copy-start.5 = (f32[16,16]{0,1:T(8,128)S(1)}, f32[16,16]{0,1:T(8,128)}, u32[]{:S(2)}) copy-start(f32[16,16]{0,1:T(8,128)} %constant.77.clone) | copy-start | bytes 3076
  0.0 6.4 %copy-start.3 = (f32[16,32,128]{2,1,0:T(8,128)S(1)}, f32[16,32,128]{2,1,0:T(8,128)}, u32[]{:S(2)}) copy-start(f32[16,32,128]{2,1,0:T(8,128)} %param.10) | copy-start | bytes 786436
  0.0 12.1 %copy-start.6 = (f32[3,2,16]{2,1,0:T(2,128)S(1)}, f32[3,2,16]{2,1,0:T(2,128)}, u32[]{:S(2)}) copy-start(f32[3,2,16]{2,1,0:T(2,128)} %param.13) | copy-start | bytes 1156
  6.4 7.7 %collective-permute-start = (f32[16,6,128]{2,1,0:T(8,128)S(1)}, f32[16,6,128]{2,1,0:T(8,128)S(1)}, u32[]{:S(2)}, u32[]{:S(2)}) collective-permute-start(f32[16,6,128]{2,1,0:T(8,128)S(1)} %get-tuple-element.21), channel_id=1, source_target_pairs={{0,1},{1,2},{2,3},{3,4},{4,5},{5,6},{6,7},{7,8},{8,9},{9,10},{10,1... | collective-permute-start | bytes 147464 | tf_op jit(solution)/shard_map/ppermute | solution.py:427
  7.0 7.1 %collective-permute-start.1 = (f32[16,6,128]{2,1,0:T(8,128)S(1)}, f32[16,6,128]{2,1,0:T(8,128)S(1)}, u32[]{:S(2)}, u32[]{:S(2)}) collective-permute-start(f32[16,6,128]{2,1,0:T(8,128)S(1)} %get-tuple-element.22), channel_id=1, source_target_pairs={{0,15},{1,0},{2,1},{3,2},{4,3},{5,4},{6,5},{7,6},{8,7},{9,8},{10,9... | collective-permute-start | bytes 147464 | tf_op jit(solution)/shard_map/ppermute | solution.py:428
  12.1 7.7 %collective-permute-start.2 = (f32[8,3,32,128]{3,2,1,0:T(8,128)}, f32[8,3,32,128]{3,2,1,0:T(8,128)S(1)}, u32[]{:S(2)}, u32[]{:S(2)}) collective-permute-start(f32[8,3,32,128]{3,2,1,0:T(8,128)} %get-tuple-element.14), channel_id=1, source_target_pairs={{0,1},{1,0},{2,3},{3,2},{4,5},{5,4},{6,7},{7,6},{8,9},{9,8},{10,11... | collective-permute-start | bytes 1179656 | tf_op jit(solution)/shard_map/ppermute | solution.py:464
  12.7 2.5 %copy-start = (f32[6,528,128]{2,1,0:T(8,128)S(1)}, f32[6,528,128]{2,1,0:T(8,128)}, u32[]{:S(2)}) copy-start(f32[6,528,128]{2,1,0:T(8,128)} %constant.75.clone.table_hbm) | copy-start | bytes 4866052
  12.7 2.5 %copy-start.1 = (f32[3,128,128]{2,1,0:T(8,128)S(1)}, f32[3,128,128]{2,1,0:T(8,128)}, u32[]{:S(2)}) copy-start(f32[3,128,128]{2,1,0:T(8,128)} %blur_ref.1) | copy-start | bytes 589828
  12.7 2.5 %copy-start.2 = (f32[3,7]{1,0:T(4,128)S(1)}, f32[3,7]{1,0:T(4,128)}, u32[]{:S(2)}) copy-start(f32[3,7]{1,0:T(4,128)} %taps_ref.1) | copy-start | bytes 256
  19.8 22.9 %collective-permute-start.8 = (f32[2,3,32,128]{3,2,1,0:T(8,128)S(1)}, f32[2,3,32,128]{3,2,1,0:T(8,128)S(1)}, u32[]{:S(2)}, u32[]{:S(2)}) collective-permute-start(f32[2,3,32,128]{3,2,1,0:T(8,128)S(1)} %fusion.17), channel_id=1, source_target_pairs={{0,12},{1,13},{2,14},{3,15},{4,8},{5,9},{6,10},{7,11},{8,4},{9,5},... | collective-permute-start | bytes 294920 | tf_op jit(solution)/shard_map/ppermute | solution.py:471
  22.1 20.7 %collective-permute-start.9 = (f32[2,3,32,128]{3,2,1,0:T(8,128)S(1)}, f32[2,3,32,128]{3,2,1,0:T(8,128)S(1)}, u32[]{:S(2)}, u32[]{:S(2)}) collective-permute-start(f32[2,3,32,128]{3,2,1,0:T(8,128)S(1)} %get-tuple-element.15), channel_id=1, source_target_pairs={{0,14},{1,15},{2,12},{3,13},{4,10},{5,11},{6,8},{7,9},{8,6},{9,7},... | collective-permute-start | bytes 294920 | tf_op jit(solution)/shard_map/ppermute | solution.py:471
  22.5 8.4 %collective-permute-start.3 = (f32[2,3,32,128]{3,2,1,0:T(8,128)S(1)}, f32[2,3,32,128]{3,2,1,0:T(8,128)S(1)}, u32[]{:S(2)}, u32[]{:S(2)}) collective-permute-start(f32[2,3,32,128]{3,2,1,0:T(8,128)S(1)} %get-tuple-element.16), channel_id=1, source_target_pairs={{0,2},{1,3},{2,0},{3,1},{4,6},{5,7},{6,4},{7,5},{8,10},{9,11},{10,... | collective-permute-start | bytes 294920 | tf_op jit(solution)/shard_map/ppermute | solution.py:471
  25.3 6.7 %collective-permute-start.4 = (f32[2,3,32,128]{3,2,1,0:T(8,128)S(1)}, f32[2,3,32,128]{3,2,1,0:T(8,128)S(1)}, u32[]{:S(2)}, u32[]{:S(2)}) collective-permute-start(f32[2,3,32,128]{3,2,1,0:T(8,128)S(1)} %get-tuple-element.17), channel_id=1, source_target_pairs={{0,4},{1,5},{2,6},{3,7},{4,0},{5,1},{6,2},{7,3},{8,12},{9,13},{10,... | collective-permute-start | bytes 294920 | tf_op jit(solution)/shard_map/ppermute | solution.py:471
  25.3 10.0 %collective-permute-start.5 = (f32[2,3,32,128]{3,2,1,0:T(8,128)S(1)}, f32[2,3,32,128]{3,2,1,0:T(8,128)S(1)}, u32[]{:S(2)}, u32[]{:S(2)}) collective-permute-start(f32[2,3,32,128]{3,2,1,0:T(8,128)S(1)} %get-tuple-element.18), channel_id=1, source_target_pairs={{0,6},{1,7},{2,4},{3,5},{4,2},{5,3},{6,0},{7,1},{8,14},{9,15},{10,... | collective-permute-start | bytes 294920 | tf_op jit(solution)/shard_map/ppermute | solution.py:471
  30.8 10.1 %collective-permute-start.6 = (f32[2,3,32,128]{3,2,1,0:T(8,128)S(1)}, f32[2,3,32,128]{3,2,1,0:T(8,128)S(1)}, u32[]{:S(2)}, u32[]{:S(2)}) collective-permute-start(f32[2,3,32,128]{3,2,1,0:T(8,128)S(1)} %get-tuple-element.19), channel_id=1, source_target_pairs={{0,8},{1,9},{2,10},{3,11},{4,12},{5,13},{6,14},{7,15},{8,0},{9,1},... | collective-permute-start | bytes 294920 | tf_op jit(solution)/shard_map/ppermute | solution.py:471
  32.0 10.8 %collective-permute-start.7 = (f32[2,3,32,128]{3,2,1,0:T(8,128)S(1)}, f32[2,3,32,128]{3,2,1,0:T(8,128)S(1)}, u32[]{:S(2)}, u32[]{:S(2)}) collective-permute-start(f32[2,3,32,128]{3,2,1,0:T(8,128)S(1)} %get-tuple-element.20), channel_id=1, source_target_pairs={{0,10},{1,11},{2,8},{3,9},{4,14},{5,15},{6,12},{7,13},{8,2},{9,3},... | collective-permute-start | bytes 294920 | tf_op jit(solution)/shard_map/ppermute | solution.py:471

commit v2 on v1

--- a/solution.py
+++ b/solution.py
@@ -75,29 +75,21 @@
     return acc
 
 
-def band_rows(mixed, images, taps, table, weight, band, begin, step):
-    at = pl.ds(begin + (table.shape[1] - mixed.shape[1]) // 2 + PAD, step)
+def band_rows(mixed, images, taps, patterns, weight, band, begin, step):
     parts = [wide(blurred(mixed, image, cut, begin, step)) for image, cut in zip(images, taps)]
     product = narrow(wide_dot(jnp.concatenate(parts, axis=0), weight))
-    acc = None
-    for orient in range(len(images) // 2):
-        cos_pattern, sin_pattern = harmonic_of(
-            table[2 * orient, at, :], table[2 * orient + 1, at, :], band
-        )
-        even = product[2 * orient * step : (2 * orient + 1) * step]
-        odd = product[(2 * orient + 1) * step : (2 * orient + 2) * step]
-        term = cos_pattern * even - sin_pattern * odd
-        acc = term if acc is None else acc + term
-    return acc
-
-
-def put(out, index, band, values):
+    cos_pattern, sin_pattern = harmonic_of(*patterns, band)
+    return cos_pattern * product[:step] - sin_pattern * product[step:]
+
+
+def put(out, index, band, values, add):
     width = out.shape[3]
     cores = out.shape[1]
     shares = values.shape[0] // width
     for share in range(shares):
         rows = values[share * width : (share + 1) * width]
-        out[index * (shares // cores) + share // cores, share % cores, band] = rows
+        at = index * (shares // cores) + share // cores, share % cores, band
+        out[at] = out[at] + rows if add else rows
 
 
 def scaled_taps(taps_ref, band, scale):
@@ -113,11 +105,14 @@
 
     orients, phases = raw.shape[0], raw.shape[1]
     loop_width = raw.shape[2]
-    bands = out.shape[2]
+    bands, width = out.shape[2], out.shape[3]
     core = lax.axis_index("gz") % 2
     phase_copy = pltpu.make_async_copy(phase_hbm, phase_ref, side_sems.at[0])
     phase_copy.start()
+    taps_copy = pltpu.make_async_copy(taps_hbm, taps_ref, side_sems.at[1])
+    taps_copy.start()
     copies = []
+    table_copies = []
     for orient in range(orients):
         row = []
         for index in range(phases):
@@ -129,18 +124,31 @@
             copy.start()
             row.append(copy)
         copies.append(row)
-    taps_copy = pltpu.make_async_copy(taps_hbm, taps_ref, side_sems.at[1])
-    taps_copy.start()
-    blur_copy = pltpu.make_async_copy(blur_hbm, blur_rows, side_sems.at[2])
-    blur_copy.start()
-    table_copy = pltpu.make_async_copy(table_hbm, table, side_sems.at[3])
-    table_copy.start()
+        if not orient:
+            blur_copy = pltpu.make_async_copy(blur_hbm, blur_rows, side_sems.at[2])
+            blur_copy.start()
+        pair = pl.ds(2 * orient, 2)
+        copy = pltpu.make_async_copy(table_hbm.at[pair], table.at[pair], side_sems.at[3 + orient])
+        copy.start()
+        table_copies.append(copy)
     step = loop_width // 2
     reach = (taps_ref.shape[1] - 1) // 2
     total = 4 * orients
     count = orients * phases
     first_sine, second_sine = math.sin(2 * math.pi / 5), math.sin(4 * math.pi / 5)
     ratio = second_sine / first_sine
+    step_chips = step // width // out.shape[1]
+
+    def half_of(at):
+        return (core + at) % 2 if len(targets) > 1 else 0
+
+    def ship(index, band):
+        chips = pl.ds(index * step_chips, step_chips)
+        for at, target in enumerate(targets):
+            pltpu.make_async_copy(
+                out.at[chips, half_of(at), band], target.at[chips, band], out_sems.at[at, band]
+            ).start()
+
     phase_copy.wait()
     for orient in range(orients):
         holder = []
@@ -176,62 +184,63 @@
             return carry
 
         lax.fori_loop(0, loop_width // step, mix, 0)
-    for image in range(total + 1):
-        mixed[image, PAD - reach : PAD, :] = mixed[
-            image, loop_width + PAD - reach : loop_width + PAD, :
+        ring_images = [2 * orient, 2 * orient + 1]
+        ring_images += [2 * orients + image for image in ring_images]
+        if orient == orients - 1:
+            ring_images.append(total)
+        for image in ring_images:
+            mixed[image, PAD - reach : PAD, :] = mixed[
+                image, loop_width + PAD - reach : loop_width + PAD, :
+            ]
+            mixed[image, loop_width + PAD : loop_width + PAD + reach, :] = mixed[
+                image, PAD : PAD + reach, :
+            ]
+        if not orient:
+            taps_copy.wait()
+            blur_copy.wait()
+            for band in range(bands):
+                weight[band] = weights(blur_rows[band])
+            plain_taps = scaled_taps(taps_ref, 0, 1.0 / count)
+            even_scale = data_scale / (4.0 * count)
+            odd_scale = data_scale * first_sine / count
+        if orient == orients - 1:
+
+            def plain_out(index, carry):
+                begin = pl.multiple_of(index * step, step)
+                rows = blurred(mixed, total, plain_taps, begin, step)
+                put(out, index, 0, narrow(wide_dot(wide(rows), weight[0])), False)
+                ship(index, 0)
+                return carry
+
+            lax.fori_loop(0, loop_width // step, plain_out, 0)
+        table_copies[orient].wait()
+        taps = [
+            [scaled_taps(taps_ref, band, even_scale), scaled_taps(taps_ref, band, odd_scale)]
+            for band in range(1, bands)
         ]
-        mixed[image, loop_width + PAD : loop_width + PAD + reach, :] = mixed[
-            image, PAD : PAD + reach, :
-        ]
-    taps_copy.wait()
-    blur_copy.wait()
-    for band in range(bands):
-        weight[band] = weights(blur_rows[band])
-    even_scale, odd_scale = data_scale / (4.0 * count), data_scale * first_sine / count
-    taps = [scaled_taps(taps_ref, 0, 1.0 / count)]
-    for band in range(1, bands):
-        taps.append(
-            [scaled_taps(taps_ref, band, even_scale), scaled_taps(taps_ref, band, odd_scale)]
-            * orients
-        )
-
-    def plain_out(index, carry):
-        begin = pl.multiple_of(index * step, step)
-        rows = blurred(mixed, total, taps[0], begin, step)
-        put(out, index, 0, narrow(wide_dot(wide(rows), weight[0])))
-        return carry
-
-    lax.fori_loop(0, loop_width // step, plain_out, 0)
-    out_copies = []
-
-    def ship(band):
-        for at, target in enumerate(targets):
-            half = (core + at) % 2 if len(targets) > 1 else 0
-            copy = pltpu.make_async_copy(
-                out.at[:, half, band], target.at[:, band], out_sems.at[at, band]
-            )
-            copy.start()
-            out_copies.append(copy)
-
-    ship(0)
-    table_copy.wait()
-    for band in range(1, bands):
-        images = list(range(2 * orients * (band - 1), 2 * orients * band))
 
         def band_out(index, carry):
             begin = pl.multiple_of(index * step, step)
-            put(
-                out,
-                index,
-                band,
-                band_rows(mixed, images, taps[band], table, weight[band], band, begin, step),
-            )
+            at = pl.ds(begin + (table.shape[1] - loop_width) // 2, step)
+            patterns = table[2 * orient, at, :], table[2 * orient + 1, at, :]
+            for band in range(1, bands):
+                base = 2 * (orients * (band - 1) + orient)
+                images = base, base + 1
+                rows = band_rows(
+                    mixed, images, taps[band - 1], patterns, weight[band], band, begin, step
+                )
+                put(out, index, band, rows, orient > 0)
+                if orient == orients - 1:
+                    ship(index, band)
             return carry
 
         lax.fori_loop(0, loop_width // step, band_out, 0)
-        ship(band)
-    for copy in out_copies:
-        copy.wait()
+    for band in range(bands):
+        for at, target in enumerate(targets):
+            half = half_of(at)
+            pltpu.make_async_copy(
+                out.at[:, half, band], target.at[:, band], out_sems.at[at, band]
+            ).wait()
 
 
 def data_sums(frames, phase_index, row_blur, column_taps, table, chunks, cores):
@@ -258,7 +267,7 @@
             pltpu.SMEM(phase_index.shape, jnp.int32),
             pltpu.SMEM(column_taps.shape, jnp.float32),
             pltpu.SemaphoreType.DMA((orients, phases)),
-            pltpu.SemaphoreType.DMA((4,)),
+            pltpu.SemaphoreType.DMA((3 + orients,)),
             pltpu.SemaphoreType.DMA((cores, bands)),
         ],
         cost_estimate=pl.CostEstimate(

time: 44.3 us -> 44.5 us (level)
  no operation moved by 1% of the time
where the time goes in v2:
time: 44.5 us; the launch traced here: 44.4 us
  starting transfers between devices  14.8 us (33%)
  waiting for transfers between devices  13.6 us (31%)
  Pallas kernels  12.5 us (28%)
  other arithmetic  1.43 us (3%)
  matrix products  1.37 us (3%)
    ppermute x7, waiting for transfers between devices, exchange(): part = lax.ppermute(part, 'gz', [(s, s ^ 2 * bit) for s in range(ring)])  13.6 us
    ppermute x7, starting transfers between devices, exchange(): part = lax.ppermute(part, 'gz', [(s, s ^ 2 * bit) for s in range(ring)])  9.21 us
    pallas_call x1, Pallas kernels, data_sums(): pl.pallas_call(data_kernel, out_shape=[jax.ShapeDtypeStruct((chunks // co...  6.69 us
    ppermute x1, starting transfers between devices, halo(): rights.append(lax.ppermute(estimate[:, :take], 'gz', back))  5.05 us
    pallas_call x1, Pallas kernels, estimate_part(): pl.pallas_call(estimate_kernel, out_shape=jax.ShapeDtypeStruct((width, pl...  4.54 us
    pallas_call x1, Pallas kernels, combine(): pl.pallas_call(combine_kernel, out_shape=jax.ShapeDtypeStruct((planes * w...  1.32 us
    neg x1, other arithmetic, exchange(): mine = lax.optimization_barrier(-mine)  1.15 us
    dot_general x1, matrix products, exact_dot(): jnp.dot(left_side, right_side, preferred_element_type=jnp.float32, precis...  0.99 us
  transfers between devices with their start and end apart: 10, of which 5 were waited for; matrix products, arithmetic and copies ran while one was open for 7% of the time, Pallas kernels for 10%

profile of v2, /device:TPU:0, one launch (start us, length us, event | category | flops | bytes accessed | tf_op | source)
XLA Modules:
  0.0 44.4 jit_solution(6442714811792744551)
XLA Ops:
  0.0 0.0 copy-start.4
  0.0 0.0 copy-start.5
  0.0 0.0 copy-start.3
  0.0 0.0 copy-start.6
  0.0 6.7 %data_sums.1 = (f32[8,3,32,128]{3,2,1,0:T(8,128)}, f32[8,3,32,128]{3,2,1,0:T(8,128)}) custom-call(s32[3,5]{1,0:T(4,128)} %phase_hbm.1, f32[3,7]{1,0:T(4,128)} %taps_ref.1, s32[3,5,1,512,128]{4,3,2,1,0:T(8,128)} %frames_hbm.1, f32[3,128,128]{2,1,0:T(8,128)} %blur_ref.1, f32[6,528,128]{2,1,0:T(8,128)} %constant.75.clone.table_hbm), custom_call_target="tpu_custom_call" | custom-call | flops 872415232 | bytes 3932160 | tf_op jit(solution)/shard_map/data_sums/pallas_call | solution.py:251
  6.7 0.0 copy-done.3
  6.7 0.6 %collective-permute-start = (f32[16,6,128]{2,1,0:T(8,128)S(1)}, f32[16,6,128]{2,1,0:T(8,128)S(1)}, u32[]{:S(2)}, u32[]{:S(2)}) collective-permute-start(f32[16,6,128]{2,1,0:T(8,128)S(1)} %get-tuple-element.21), channel_id=1, source_target_pairs={{0,1},{1,2},{2,3},{3,4},{4,5},{5,6},{6,7},{7,8},{8,9},{9,10},{10,1... | collective-permute-start | bytes 147464 | tf_op jit(solution)/shard_map/ppermute | solution.py:436
  7.3 5.0 %collective-permute-start.1 = (f32[16,6,128]{2,1,0:T(8,128)S(1)}, f32[16,6,128]{2,1,0:T(8,128)S(1)}, u32[]{:S(2)}, u32[]{:S(2)}) collective-permute-start(f32[16,6,128]{2,1,0:T(8,128)S(1)} %get-tuple-element.22), channel_id=1, source_target_pairs={{0,15},{1,0},{2,1},{3,2},{4,3},{5,4},{6,5},{7,6},{8,7},{9,8},{10,9... | collective-permute-start | bytes 147464 | tf_op jit(solution)/shard_map/ppermute | solution.py:437
  12.3 0.0 collective-permute-start.2
  12.3 0.0 copy-done.6
  12.4 0.1 fusion.34
  12.5 0.0 copy-done.4
  12.5 0.0 copy-done.5
  12.5 0.2 fusion.18
  12.8 0.2 convolution_bitcast_fusion.1
  13.0 0.0 copy-start
  13.0 0.0 copy-start.1
  13.0 0.0 copy-start.2
  13.0 0.1 copy.12
  13.1 0.1 copy.14.adjoint_ref
  13.2 1.1 %neg.6 = f32[8,3,32,128]{3,2,1,0:T(8,128)S(1)} negate(f32[8,3,32,128]{3,2,1,0:T(8,128)} %get-tuple-element.13) | non-fusion elementwise | flops 98304 | bytes 786432 | tf_op jit(solution)/shard_map/neg | solution.py:474
  14.4 0.0 collective-permute-done
  14.4 0.0 collective-permute-done.1
  14.5 1.0 %convolution_bitcast_fusion.axial_ref = f32[3,44,16,128]{3,2,1,0:T(8,128)S(1)} fusion(f32[3,16,16,1]{2,1,3,0:T(8,128)S(1)} %convolution_bitcast_fusion.1, f32[2,8,44,128]{3,2,1,0:T(8,128)S(1)} %bitcast.62), kind=kOutput, calls=%fused_computation.16 | convolution fusion | flops 51904512 | bytes 1444864 | tf_op jit(solution)/shard_map/dot_general | solution.py:19
  15.5 0.0 copy-done
  15.5 0.0 copy-done.1
  15.5 0.0 copy-done.2
  15.5 4.5 %estimate_part.1.estimate_ref = f32[32,16,128]{2,1,0:T(8,128)S(1)} custom-call(f32[3,7]{1,0:T(4,128)S(1)} %copy-done.2, f32[3,44,16,128]{3,2,1,0:T(8,128)S(1)} %convolution_bitcast_fusion.axial_ref, f32[6,528,128]{2,1,0:T(8,128)S(1)} %copy-done, f32[3,128,128]{2,1,0:T(8,128)S(1)} %copy-done.1), custom_call_target="tpu_custom_call" | custom-call | flops 16106127360 | bytes 1081344 | tf_op jit(solution)/shard_map/estimate_part/pallas_call | solution.py:377
  20.0 0.0 collective-permute-done.2
  20.1 2.2 %collective-permute-start.8 = (f32[2,3,32,128]{3,2,1,0:T(8,128)S(1)}, f32[2,3,32,128]{3,2,1,0:T(8,128)S(1)}, u32[]{:S(2)}, u32[]{:S(2)}) collective-permute-start(f32[2,3,32,128]{3,2,1,0:T(8,128)S(1)} %fusion.17), channel_id=1, source_target_pairs={{0,12},{1,13},{2,14},{3,15},{4,8},{5,9},{6,10},{7,11},{8,4},{9,5},... | collective-permute-start | bytes 294920 | tf_op jit(solution)/shard_map/ppermute | solution.py:480
  22.4 0.3 collective-permute-start.9
  22.8 2.8 %collective-permute-start.3 = (f32[2,3,32,128]{3,2,1,0:T(8,128)S(1)}, f32[2,3,32,128]{3,2,1,0:T(8,128)S(1)}, u32[]{:S(2)}, u32[]{:S(2)}) collective-permute-start(f32[2,3,32,128]{3,2,1,0:T(8,128)S(1)} %get-tuple-element.16), channel_id=1, source_target_pairs={{0,2},{1,3},{2,0},{3,1},{4,6},{5,7},{6,4},{7,5},{8,10},{9,11},{10,... | collective-permute-start | bytes 294920 | tf_op jit(solution)/shard_map/ppermute | solution.py:480
  25.6 0.0 collective-permute-start.4
  25.6 1.5 %collective-permute-start.5 = (f32[2,3,32,128]{3,2,1,0:T(8,128)S(1)}, f32[2,3,32,128]{3,2,1,0:T(8,128)S(1)}, u32[]{:S(2)}, u32[]{:S(2)}) collective-permute-start(f32[2,3,32,128]{3,2,1,0:T(8,128)S(1)} %get-tuple-element.18), channel_id=1, source_target_pairs={{0,6},{1,7},{2,4},{3,5},{4,2},{5,3},{6,0},{7,1},{8,14},{9,15},{10,... | collective-permute-start | bytes 294920 | tf_op jit(solution)/shard_map/ppermute | solution.py:480
  27.1 4.0 %collective-permute-done.3 = f32[2,3,32,128]{3,2,1,0:T(8,128)S(1)} collective-permute-done((f32[2,3,32,128]{3,2,1,0:T(8,128)S(1)}, f32[2,3,32,128]{3,2,1,0:T(8,128)S(1)}, u32[]{:S(2)}, u32[]{:S(2)}) %collective-permute-start.3) | collective-permute-done | bytes 98336 | tf_op jit(solution)/shard_map/ppermute | solution.py:480
  31.1 0.0 collective-permute-start.6
  31.1 1.2 %collective-permute-done.4 = f32[2,3,32,128]{3,2,1,0:T(8,128)S(1)} collective-permute-done((f32[2,3,32,128]{3,2,1,0:T(8,128)S(1)}, f32[2,3,32,128]{3,2,1,0:T(8,128)S(1)}, u32[]{:S(2)}, u32[]{:S(2)}) %collective-permute-start.4) | collective-permute-done | bytes 98336 | tf_op jit(solution)/shard_map/ppermute | solution.py:480
  32.3 2.3 %collective-permute-start.7 = (f32[2,3,32,128]{3,2,1,0:T(8,128)S(1)}, f32[2,3,32,128]{3,2,1,0:T(8,128)S(1)}, u32[]{:S(2)}, u32[]{:S(2)}) collective-permute-start(f32[2,3,32,128]{3,2,1,0:T(8,128)S(1)} %get-tuple-element.20), channel_id=1, source_target_pairs={{0,10},{1,11},{2,8},{3,9},{4,14},{5,15},{6,12},{7,13},{8,2},{9,3},... | collective-permute-start | bytes 294920 | tf_op jit(solution)/shard_map/ppermute | solution.py:480
  34.6 0.9 %collective-permute-done.5 = f32[2,3,32,128]{3,2,1,0:T(8,128)S(1)} collective-permute-done((f32[2,3,32,128]{3,2,1,0:T(8,128)S(1)}, f32[2,3,32,128]{3,2,1,0:T(8,128)S(1)}, u32[]{:S(2)}, u32[]{:S(2)}) %collective-permute-start.5) | collective-permute-done | bytes 98336 | tf_op jit(solution)/shard_map/ppermute | solution.py:480
  35.6 5.6 %collective-permute-done.6 = f32[2,3,32,128]{3,2,1,0:T(8,128)S(1)} collective-permute-done((f32[2,3,32,128]{3,2,1,0:T(8,128)S(1)}, f32[2,3,32,128]{3,2,1,0:T(8,128)S(1)}, u32[]{:S(2)}, u32[]{:S(2)}) %collective-permute-start.6) | collective-permute-done | bytes 98336 | tf_op jit(solution)/shard_map/ppermute | solution.py:480
  41.2 1.8 %collective-permute-done.7 = f32[2,3,32,128]{3,2,1,0:T(8,128)S(1)} collective-permute-done((f32[2,3,32,128]{3,2,1,0:T(8,128)S(1)}, f32[2,3,32,128]{3,2,1,0:T(8,128)S(1)}, u32[]{:S(2)}, u32[]{:S(2)}) %collective-permute-start.7) | collective-permute-done | bytes 98336 | tf_op jit(solution)/shard_map/ppermute | solution.py:480
  43.0 0.0 collective-permute-done.8
  43.1 0.0 collective-permute-done.9
  43.1 1.3 %combine.1 = f32[512,128]{1,0:T(8,128)} custom-call(f32[16,48]{1,0:T(8,128)S(1)} %copy.14.adjoint_ref, f32[32,16,128]{2,1,0:T(8,128)S(1)} %estimate_part.1.estimate_ref, f32[1536,128]{1,0:T(8,128)S(1)} %bitcast.58), custom_call_target="tpu_custom_call" | custom-call | flops 6291456 | bytes 786432 | tf_op jit(solution)/shard_map/combine/pallas_call | solution.py:412
  (18 shorter events, 0.3 us)
Async XLA Ops:
  0.0 12.5 %copy-start.4 = (f32[16,16]{0,1:T(8,128)S(1)}, f32[16,16]{0,1:T(8,128)}, u32[]{:S(2)}) copy-start(f32[16,16]{0,1:T(8,128)} %constant.78.clone) | copy-start | bytes 3076
  0.0 12.5 %copy-start.5 = (f32[16,16]{0,1:T(8,128)S(1)}, f32[16,16]{0,1:T(8,128)}, u32[]{:S(2)}) copy-start(f32[16,16]{0,1:T(8,128)} %constant.77.clone) | copy-start | bytes 3076
  0.0 6.7 %copy-start.3 = (f32[16,32,128]{2,1,0:T(8,128)S(1)}, f32[16,32,128]{2,1,0:T(8,128)}, u32[]{:S(2)}) copy-start(f32[16,32,128]{2,1,0:T(8,128)} %param.10) | copy-start | bytes 786436
  0.0 12.3 %copy-start.6 = (f32[3,2,16]{2,1,0:T(2,128)S(1)}, f32[3,2,16]{2,1,0:T(2,128)}, u32[]{:S(2)}) copy-start(f32[3,2,16]{2,1,0:T(2,128)} %param.13) | copy-start | bytes 1156
  6.7 7.7 %collective-permute-start = (f32[16,6,128]{2,1,0:T(8,128)S(1)}, f32[16,6,128]{2,1,0:T(8,128)S(1)}, u32[]{:S(2)}, u32[]{:S(2)}) collective-permute-start(f32[16,6,128]{2,1,0:T(8,128)S(1)} %get-tuple-element.21), channel_id=1, source_target_pairs={{0,1},{1,2},{2,3},{3,4},{4,5},{5,6},{6,7},{7,8},{8,9},{9,10},{10,1... | collective-permute-start | bytes 147464 | tf_op jit(solution)/shard_map/ppermute | solution.py:436
  7.3 7.1 %collective-permute-start.1 = (f32[16,6,128]{2,1,0:T(8,128)S(1)}, f32[16,6,128]{2,1,0:T(8,128)S(1)}, u32[]{:S(2)}, u32[]{:S(2)}) collective-permute-start(f32[16,6,128]{2,1,0:T(8,128)S(1)} %get-tuple-element.22), channel_id=1, source_target_pairs={{0,15},{1,0},{2,1},{3,2},{4,3},{5,4},{6,5},{7,6},{8,7},{9,8},{10,9... | collective-permute-start | bytes 147464 | tf_op jit(solution)/shard_map/ppermute | solution.py:437
  12.3 7.7 %collective-permute-start.2 = (f32[8,3,32,128]{3,2,1,0:T(8,128)}, f32[8,3,32,128]{3,2,1,0:T(8,128)S(1)}, u32[]{:S(2)}, u32[]{:S(2)}) collective-permute-start(f32[8,3,32,128]{3,2,1,0:T(8,128)} %get-tuple-element.14), channel_id=1, source_target_pairs={{0,1},{1,0},{2,3},{3,2},{4,5},{5,4},{6,7},{7,6},{8,9},{9,8},{10,11... | collective-permute-start | bytes 1179656 | tf_op jit(solution)/shard_map/ppermute | solution.py:473
  13.0 2.5 %copy-start = (f32[6,528,128]{2,1,0:T(8,128)S(1)}, f32[6,528,128]{2,1,0:T(8,128)}, u32[]{:S(2)}) copy-start(f32[6,528,128]{2,1,0:T(8,128)} %constant.75.clone.table_hbm) | copy-start | bytes 4866052
  13.0 2.5 %copy-start.1 = (f32[3,128,128]{2,1,0:T(8,128)S(1)}, f32[3,128,128]{2,1,0:T(8,128)}, u32[]{:S(2)}) copy-start(f32[3,128,128]{2,1,0:T(8,128)} %blur_ref.1) | copy-start | bytes 589828
  13.0 2.5 %copy-start.2 = (f32[3,7]{1,0:T(4,128)S(1)}, f32[3,7]{1,0:T(4,128)}, u32[]{:S(2)}) copy-start(f32[3,7]{1,0:T(4,128)} %taps_ref.1) | copy-start | bytes 256
  20.1 22.9 %collective-permute-start.8 = (f32[2,3,32,128]{3,2,1,0:T(8,128)S(1)}, f32[2,3,32,128]{3,2,1,0:T(8,128)S(1)}, u32[]{:S(2)}, u32[]{:S(2)}) collective-permute-start(f32[2,3,32,128]{3,2,1,0:T(8,128)S(1)} %fusion.17), channel_id=1, source_target_pairs={{0,12},{1,13},{2,14},{3,15},{4,8},{5,9},{6,10},{7,11},{8,4},{9,5},... | collective-permute-start | bytes 294920 | tf_op jit(solution)/shard_map/ppermute | solution.py:480
  22.4 20.7 %collective-permute-start.9 = (f32[2,3,32,128]{3,2,1,0:T(8,128)S(1)}, f32[2,3,32,128]{3,2,1,0:T(8,128)S(1)}, u32[]{:S(2)}, u32[]{:S(2)}) collective-permute-start(f32[2,3,32,128]{3,2,1,0:T(8,128)S(1)} %get-tuple-element.15), channel_id=1, source_target_pairs={{0,14},{1,15},{2,12},{3,13},{4,10},{5,11},{6,8},{7,9},{8,6},{9,7},... | collective-permute-start | bytes 294920 | tf_op jit(solution)/shard_map/ppermute | solution.py:480
  22.8 8.3 %collective-permute-start.3 = (f32[2,3,32,128]{3,2,1,0:T(8,128)S(1)}, f32[2,3,32,128]{3,2,1,0:T(8,128)S(1)}, u32[]{:S(2)}, u32[]{:S(2)}) collective-permute-start(f32[2,3,32,128]{3,2,1,0:T(8,128)S(1)} %get-tuple-element.16), channel_id=1, source_target_pairs={{0,2},{1,3},{2,0},{3,1},{4,6},{5,7},{6,4},{7,5},{8,10},{9,11},{10,... | collective-permute-start | bytes 294920 | tf_op jit(solution)/shard_map/ppermute | solution.py:480
  25.6 6.7 %collective-permute-start.4 = (f32[2,3,32,128]{3,2,1,0:T(8,128)S(1)}, f32[2,3,32,128]{3,2,1,0:T(8,128)S(1)}, u32[]{:S(2)}, u32[]{:S(2)}) collective-permute-start(f32[2,3,32,128]{3,2,1,0:T(8,128)S(1)} %get-tuple-element.17), channel_id=1, source_target_pairs={{0,4},{1,5},{2,6},{3,7},{4,0},{5,1},{6,2},{7,3},{8,12},{9,13},{10,... | collective-permute-start | bytes 294920 | tf_op jit(solution)/shard_map/ppermute | solution.py:480
  25.6 10.0 %collective-permute-start.5 = (f32[2,3,32,128]{3,2,1,0:T(8,128)S(1)}, f32[2,3,32,128]{3,2,1,0:T(8,128)S(1)}, u32[]{:S(2)}, u32[]{:S(2)}) collective-permute-start(f32[2,3,32,128]{3,2,1,0:T(8,128)S(1)} %get-tuple-element.18), channel_id=1, source_target_pairs={{0,6},{1,7},{2,4},{3,5},{4,2},{5,3},{6,0},{7,1},{8,14},{9,15},{10,... | collective-permute-start | bytes 294920 | tf_op jit(solution)/shard_map/ppermute | solution.py:480
  31.1 10.1 %collective-permute-start.6 = (f32[2,3,32,128]{3,2,1,0:T(8,128)S(1)}, f32[2,3,32,128]{3,2,1,0:T(8,128)S(1)}, u32[]{:S(2)}, u32[]{:S(2)}) collective-permute-start(f32[2,3,32,128]{3,2,1,0:T(8,128)S(1)} %get-tuple-element.19), channel_id=1, source_target_pairs={{0,8},{1,9},{2,10},{3,11},{4,12},{5,13},{6,14},{7,15},{8,0},{9,1},... | collective-permute-start | bytes 294920 | tf_op jit(solution)/shard_map/ppermute | solution.py:480
  32.3 10.7 %collective-permute-start.7 = (f32[2,3,32,128]{3,2,1,0:T(8,128)S(1)}, f32[2,3,32,128]{3,2,1,0:T(8,128)S(1)}, u32[]{:S(2)}, u32[]{:S(2)}) collective-permute-start(f32[2,3,32,128]{3,2,1,0:T(8,128)S(1)} %get-tuple-element.20), channel_id=1, source_target_pairs={{0,10},{1,11},{2,8},{3,9},{4,14},{5,15},{6,12},{7,13},{8,2},{9,3},... | collective-permute-start | bytes 294920 | tf_op jit(solution)/shard_map/ppermute | solution.py:480

commit v3 on v1

--- a/solution.py
+++ b/solution.py
@@ -135,7 +135,7 @@
     blur_copy.start()
     table_copy = pltpu.make_async_copy(table_hbm, table, side_sems.at[3])
     table_copy.start()
-    step = loop_width // 2
+    step = loop_width
     reach = (taps_ref.shape[1] - 1) // 2
     total = 4 * orients
     count = orients * phases
@@ -462,11 +462,16 @@
     chip = lax.axis_index("gz") // 2
     mine, other = sums
     other = lax.ppermute(other, "gz", [(s, s ^ 1) for s in range(ring)])
-    mine = lax.optimization_barrier(-mine)
-    both = jnp.stack([mine, -other], axis=1)
+    early = ring // 4
+    first = lax.dynamic_index_in_dim(mine, chip ^ early, 0, keepdims=False)
+    first = lax.optimization_barrier(-first)
     parts = []
     for bit in range(ring // 2):
-        part = lax.dynamic_index_in_dim(both, chip ^ bit, 0, keepdims=False)
+        own = first
+        if bit != early:
+            own = -lax.dynamic_index_in_dim(mine, chip ^ bit, 0, keepdims=False)
+        got = -lax.dynamic_index_in_dim(other, chip ^ bit, 0, keepdims=False)
+        part = jnp.stack([own, got])
         if bit:
             part = lax.ppermute(part, "gz", [(s, s ^ (2 * bit)) for s in range(ring)])
         parts.append(part)

time: 44.3 us -> 45.3 us (1.023)
  waiting for transfers between devices: 13.6 us -> 8.72 us
  local copies, waits for them, and re-layouts: 0.28 us -> 2.3 us
  other arithmetic: 1.43 us -> 2.95 us
  matrix products: 1.37 us -> 2.71 us
  starting transfers between devices: 14.8 us -> 16.1 us
    ppermute x7, waiting for transfers between devices: 13.6 us -> 8.71 us  [exchange(): part = lax.ppermute(part, 'gz', [(s, s ^ 2 * bit) for s in range(ring)])]
    concatenate x1, other arithmetic: 0.04 us -> 0.92 us  [shards(): extended = jnp.concatenate(pieces, axis=1)]
    reshape x2, local copies, waits for them, and re-layouts: 0.08 us -> 0.84 us  [combine(): adjoint = forward.transpose(2, 1, 0).reshape(planes, depth)]
    dot_general x1, matrix products: 0.99 us -> 1.72 us  [exact_dot(): jnp.dot(left_side, right_side, preferred_element_type=jnp.float32, precis...]
    ppermute x7, starting transfers between devices: 9.23 us -> 9.91 us  [exchange(): part = lax.ppermute(part, 'gz', [(s, s ^ 2 * bit) for s in range(ring)])]
    neg x1 -> x2, other arithmetic: 1.15 us -> 1.82 us  [the longest x1 1.77 us: exchange(): own = -lax.dynamic_index_in_dim(mine, chip ^ bit, 0, keepdims=False)]
    slice x1, local copies, waits for them, and re-layouts: 0.01 us -> 0.67 us  [halo(): lefts.insert(0, lax.ppermute(estimate[:, width - take:], 'gz', forth))]
    dot_general x1, matrix products: 0.16 us -> 0.77 us  [shards(): jnp.einsum('mzw,mzv->mwv', forward, forward, precision=lax.Precision.HIGH...]
  transfers between devices with their start and end apart: 10 -> 10, of which waited for: 5 -> 4; matrix products, arithmetic and copies ran while one was open for 7% -> 17% of each run, Pallas kernels for 10% -> 10%
where the time goes in v3:
time: 45.3 us; the launch traced here: 45 us
  starting transfers between devices  16.1 us (36%)
  Pallas kernels  11.9 us (26%)
  waiting for transfers between devices  8.72 us (19%)
  other arithmetic  2.95 us (7%)
  matrix products  2.71 us (6%)
  local copies, waits for them, and re-layouts  2.3 us (5%)
    ppermute x7, starting transfers between devices, exchange(): part = lax.ppermute(part, 'gz', [(s, s ^ 2 * bit) for s in range(ring)])  9.91 us
    ppermute x7, waiting for transfers between devices, exchange(): part = lax.ppermute(part, 'gz', [(s, s ^ 2 * bit) for s in range(ring)])  8.71 us
    pallas_call x1, Pallas kernels, data_sums(): pl.pallas_call(data_kernel, out_shape=[jax.ShapeDtypeStruct((chunks // co...  6.05 us
    ppermute x1, starting transfers between devices, halo(): rights.append(lax.ppermute(estimate[:, :take], 'gz', back))  5.64 us
    pallas_call x1, Pallas kernels, estimate_part(): pl.pallas_call(estimate_kernel, out_shape=jax.ShapeDtypeStruct((width, pl...  4.54 us
    neg x1, other arithmetic, exchange(): own = -lax.dynamic_index_in_dim(mine, chip ^ bit, 0, keepdims=False)  1.77 us
    dot_general x1, matrix products, exact_dot(): jnp.dot(left_side, right_side, preferred_element_type=jnp.float32, precis...  1.72 us
    pallas_call x1, Pallas kernels, combine(): pl.pallas_call(combine_kernel, out_shape=jax.ShapeDtypeStruct((planes * w...  1.32 us
  transfers between devices with their start and end apart: 10, of which 4 were waited for; matrix products, arithmetic and copies ran while one was open for 17% of the time, Pallas kernels for 10%

profile of v3, /device:TPU:0, one launch (start us, length us, event | category | flops | bytes accessed | tf_op | source)
XLA Modules:
  0.0 45.0 jit_solution(6477715617508844008)
XLA Ops:
  0.0 0.0 copy-start.6
  0.0 6.0 %data_sums.1 = (f32[8,3,32,128]{3,2,1,0:T(8,128)}, f32[8,3,32,128]{3,2,1,0:T(8,128)}) custom-call(s32[3,5]{1,0:T(4,128)} %phase_hbm.1, f32[3,7]{1,0:T(4,128)} %taps_ref.1, s32[3,5,1,512,128]{4,3,2,1,0:T(8,128)} %frames_hbm.1, f32[3,128,128]{2,1,0:T(8,128)} %blur_ref.1, f32[6,528,128]{2,1,0:T(8,128)} %constant.91.clone.table_hbm), custom_call_target="tpu_custom_call" | custom-call | flops 872415232 | bytes 3932160 | tf_op jit(solution)/shard_map/data_sums/pallas_call | solution.py:242
  6.1 0.6 %collective-permute-start.2 = (f32[8,3,32,128]{3,2,1,0:T(8,128)}, f32[8,3,32,128]{3,2,1,0:T(8,128)S(1)}, u32[]{:S(2)}, u32[]{:S(2)}) collective-permute-start(f32[8,3,32,128]{3,2,1,0:T(8,128)} %get-tuple-element.14), channel_id=1, source_target_pairs={{0,1},{1,0},{2,3},{3,2},{4,5},{5,4},{6,7},{7,6},{8,9},{9,8},{10,11... | collective-permute-start | bytes 1179656 | tf_op jit(solution)/shard_map/ppermute | solution.py:464
  6.6 0.0 copy-done.3
  6.6 0.7 %fusion.20 = (f32[16,6,128]{2,1,0:T(8,128)}, f32[16,6,128]{2,1,0:T(8,128)}) fusion(f32[16,32,128]{2,1,0:T(8,128)S(1)} %copy-done.3), kind=kLoop, calls=%fused_computation.64 | loop fusion | bytes 196608 | tf_op jit(solution)/shard_map/slice | solution.py:427
  7.3 0.0 collective-permute-start
  7.3 5.6 %collective-permute-start.1 = (f32[16,6,128]{2,1,0:T(8,128)}, f32[16,6,128]{2,1,0:T(8,128)}, u32[]{:S(2)}, u32[]{:S(2)}) collective-permute-start(f32[16,6,128]{2,1,0:T(8,128)} %get-tuple-element.32), channel_id=1, source_target_pairs={{0,15},{1,0},{2,1},{3,2},{4,3},{5,4},{6,5},{7,6},{8,7},{9,8},{10,9... | collective-permute-start | bytes 147464 | tf_op jit(solution)/shard_map/ppermute | solution.py:428
  13.0 0.0 copy-done.8
  13.0 0.1 fusion.17
  13.2 0.0 copy-done.6
  13.2 0.0 copy-done.7
  13.2 0.2 fusion.1
  13.4 0.0 copy-start
  13.4 0.0 copy-start.1
  13.5 0.0 copy-start.2
  13.5 1.8 %dynamic-slice_negate_fusion.1 = (f32[1,3,32,128]{3,2,1,0:T(8,128)S(1)}, f32[1,3,32,128]{3,2,1,0:T(8,128)S(1)}, f32[1,3,32,128]{3,2,1,0:T(8,128)S(1)}, f32[3,32,...) fusion(f32[8,3,32,128]{3,2,1,0:T(8,128)} %get-tuple-element.13,, ...), kind=kLoop, calls=%fused_computation.14 | loop fusion | flops 98303 | bytes 786464 | tf_op jit(solution)/shard_map/neg | solution.py:472
  15.2 0.8 %convolution_bitcast_fusion.1 = f32[3,16,16,1]{2,1,3,0:T(8,128)} fusion(f32[3,16,16]{2,1,0:T(8,128)S(1)} %fusion.1), kind=kOutput, calls=%fused_computation.1 | convolution fusion | flops 147456 | bytes 6144 | tf_op jit(solution)/shard_map/mzw,mzv->mwv/dot_general | solution.py:497
  16.0 0.7 %copy.12 = f32[16,16,3]{0,2,1:T(4,128)} copy(f32[16,16,3]{1,0,2:T(8,128)S(1)} %bitcast.42) | data formatting | bytes 6144 | tf_op jit(solution)/shard_map/transpose;zk,mkw->mzw/transpose | solution.py:401
  16.7 0.8 %reshape.26 = f32[16,48]{0,1:T(8,128)S(1)} reshape(f32[16,16,3]{0,2,1:T(4,128)} %copy.12) | data formatting | bytes 6144 | tf_op jit(solution)/shard_map/reshape | solution.py:401
  17.5 0.1 copy.14.adjoint_ref
  17.5 0.0 collective-permute-done
  17.5 0.0 collective-permute-done.1
  17.5 0.9 %pad_maximum_fusion = f32[16,44,128]{2,1,0:T(8,128)S(1)} fusion(f32[16,6,128]{2,1,0:T(8,128)} %collective-permute-done.1, f32[16,32,128]{2,1,0:T(8,128)S(1)} %copy-done.3, f32[16,6,128]{2,1,0:T(8,128)} %collective-permute-done), kind=kLoop, calls=%fused_computation.2 | loop fusion | flops 180224 | bytes 720896 | tf_op jit(solution)/shard_map/concatenate | solution.py:498
  18.5 1.7 %convolution_bitcast_fusion.axial_ref = f32[3,44,16,128]{3,2,1,0:T(8,128)S(1)} fusion(f32[3,16,16,1]{2,1,3,0:T(8,128)} %convolution_bitcast_fusion.1, f32[2,8,44,128]{3,2,1,0:T(8,128)S(1)} %bitcast.41), kind=kOutput, calls=%fused_computation | convolution fusion | flops 51904512 | bytes 1444864 | tf_op jit(solution)/shard_map/dot_general | solution.py:19
  20.2 0.0 copy-done
  20.2 0.0 copy-done.1
  20.2 0.0 copy-done.2
  20.2 0.0 copy-start.5
  20.2 0.0 copy-start.4
  20.3 4.5 %estimate_part.1.estimate_ref = f32[32,16,128]{2,1,0:T(8,128)S(1)} custom-call(f32[3,7]{1,0:T(4,128)S(1)} %copy-done.2, f32[3,44,16,128]{3,2,1,0:T(8,128)S(1)} %convolution_bitcast_fusion.axial_ref, f32[6,528,128]{2,1,0:T(8,128)S(1)} %copy-done, f32[3,128,128]{2,1,0:T(8,128)S(1)} %copy-done.1), custom_call_target="tpu_custom_call" | custom-call | flops 16106127360 | bytes 1081344 | tf_op jit(solution)/shard_map/estimate_part/pallas_call | solution.py:368
  24.8 0.0 collective-permute-done.2
  24.9 0.0 copy-done.5
  24.9 0.6 %collective-permute-start.6 = (f32[2,3,32,128]{3,2,1,0:T(8,128)S(1)}, f32[2,3,32,128]{3,2,1,0:T(8,128)S(1)}, u32[]{:S(2)}, u32[]{:S(2)}) collective-permute-start(f32[2,3,32,128]{3,2,1,0:T(8,128)S(1)} %pad_maximum_fusion.4), channel_id=1, source_target_pairs={{0,8},{1,9},{2,10},{3,11},{4,12},{5,13},{6,14},{7,15},{8,0},{9,1},... | collective-permute-start | bytes 294920 | tf_op jit(solution)/shard_map/ppermute | solution.py:476
  25.5 0.0 copy-done.4
  25.6 1.7 %collective-permute-start.5 = (f32[2,3,32,128]{3,2,1,0:T(8,128)S(1)}, f32[2,3,32,128]{3,2,1,0:T(8,128)S(1)}, u32[]{:S(2)}, u32[]{:S(2)}) collective-permute-start(f32[2,3,32,128]{3,2,1,0:T(8,128)S(1)} %pad_maximum_fusion.3), channel_id=1, source_target_pairs={{0,6},{1,7},{2,4},{3,5},{4,2},{5,3},{6,0},{7,1},{8,14},{9,15},{10,... | collective-permute-start | bytes 294920 | tf_op jit(solution)/shard_map/ppermute | solution.py:476
  27.3 0.5 %collective-permute-start.4 = (f32[2,3,32,128]{3,2,1,0:T(8,128)S(1)}, f32[2,3,32,128]{3,2,1,0:T(8,128)S(1)}, u32[]{:S(2)}, u32[]{:S(2)}) collective-permute-start(f32[2,3,32,128]{3,2,1,0:T(8,128)S(1)} %pad_maximum_fusion.2), channel_id=1, source_target_pairs={{0,4},{1,5},{2,6},{3,7},{4,0},{5,1},{6,2},{7,3},{8,12},{9,13},{10,... | collective-permute-start | bytes 294920 | tf_op jit(solution)/shard_map/ppermute | solution.py:476
  27.8 1.5 %collective-permute-start.3 = (f32[2,3,32,128]{3,2,1,0:T(8,128)S(1)}, f32[2,3,32,128]{3,2,1,0:T(8,128)S(1)}, u32[]{:S(2)}, u32[]{:S(2)}) collective-permute-start(f32[2,3,32,128]{3,2,1,0:T(8,128)S(1)} %pad_maximum_fusion.1), channel_id=1, source_target_pairs={{0,2},{1,3},{2,0},{3,1},{4,6},{5,7},{6,4},{7,5},{8,10},{9,11},{10,... | collective-permute-start | bytes 294920 | tf_op jit(solution)/shard_map/ppermute | solution.py:476
  29.3 1.9 %collective-permute-start.7 = (f32[2,3,32,128]{3,2,1,0:T(8,128)S(1)}, f32[2,3,32,128]{3,2,1,0:T(8,128)S(1)}, u32[]{:S(2)}, u32[]{:S(2)}) collective-permute-start(f32[2,3,32,128]{3,2,1,0:T(8,128)S(1)} %pad_maximum_fusion.5), channel_id=1, source_target_pairs={{0,10},{1,11},{2,8},{3,9},{4,14},{5,15},{6,12},{7,13},{8,2},{9,3},... | collective-permute-start | bytes 294920 | tf_op jit(solution)/shard_map/ppermute | solution.py:476
  31.1 3.3 %collective-permute-done.3 = f32[2,3,32,128]{3,2,1,0:T(8,128)S(1)} collective-permute-done((f32[2,3,32,128]{3,2,1,0:T(8,128)S(1)}, f32[2,3,32,128]{3,2,1,0:T(8,128)S(1)}, u32[]{:S(2)}, u32[]{:S(2)}) %collective-permute-start.3) | collective-permute-done | bytes 98336 | tf_op jit(solution)/shard_map/ppermute | solution.py:476
  34.4 1.8 %collective-permute-start.8 = (f32[2,3,32,128]{3,2,1,0:T(8,128)S(1)}, f32[2,3,32,128]{3,2,1,0:T(8,128)S(1)}, u32[]{:S(2)}, u32[]{:S(2)}) collective-permute-start(f32[2,3,32,128]{3,2,1,0:T(8,128)S(1)} %pad_maximum_fusion.6), channel_id=1, source_target_pairs={{0,12},{1,13},{2,14},{3,15},{4,8},{5,9},{6,10},{7,11},{8,4},{9,5},... | collective-permute-start | bytes 294920 | tf_op jit(solution)/shard_map/ppermute | solution.py:476
  36.2 0.0 collective-permute-done.4
  36.2 2.0 %collective-permute-start.9 = (f32[2,3,32,128]{3,2,1,0:T(8,128)S(1)}, f32[2,3,32,128]{3,2,1,0:T(8,128)S(1)}, u32[]{:S(2)}, u32[]{:S(2)}) collective-permute-start(f32[2,3,32,128]{3,2,1,0:T(8,128)S(1)} %pad_maximum_fusion.7), channel_id=1, source_target_pairs={{0,14},{1,15},{2,12},{3,13},{4,10},{5,11},{6,8},{7,9},{8,6},{9,7},... | collective-permute-start | bytes 294920 | tf_op jit(solution)/shard_map/ppermute | solution.py:476
  38.2 0.0 collective-permute-done.5
  38.2 0.0 collective-permute-done.6
  38.2 0.3 collective-permute-done.7
  38.5 2.9 %collective-permute-done.8 = f32[2,3,32,128]{3,2,1,0:T(8,128)S(1)} collective-permute-done((f32[2,3,32,128]{3,2,1,0:T(8,128)S(1)}, f32[2,3,32,128]{3,2,1,0:T(8,128)S(1)}, u32[]{:S(2)}, u32[]{:S(2)}) %collective-permute-start.8) | collective-permute-done | bytes 98336 | tf_op jit(solution)/shard_map/ppermute | solution.py:476
  41.4 2.3 %collective-permute-done.9 = f32[2,3,32,128]{3,2,1,0:T(8,128)S(1)} collective-permute-done((f32[2,3,32,128]{3,2,1,0:T(8,128)S(1)}, f32[2,3,32,128]{3,2,1,0:T(8,128)S(1)}, u32[]{:S(2)}, u32[]{:S(2)}) %collective-permute-start.9) | collective-permute-done | bytes 98336 | tf_op jit(solution)/shard_map/ppermute | solution.py:476
  43.7 1.3 %combine.1 = f32[512,128]{1,0:T(8,128)} custom-call(f32[16,48]{1,0:T(8,128)S(1)} %copy.14.adjoint_ref, f32[32,16,128]{2,1,0:T(8,128)S(1)} %estimate_part.1.estimate_ref, f32[1536,128]{1,0:T(8,128)S(1)} %bitcast.40), custom_call_target="tpu_custom_call" | custom-call | flops 6291456 | bytes 786432 | tf_op jit(solution)/shard_map/combine/pallas_call | solution.py:403
  (22 shorter events, 0.2 us)
Async XLA Ops:
  0.0 13.2 %copy-start.6 = (f32[16,16]{0,1:T(8,128)S(1)}, f32[16,16]{0,1:T(8,128)}, u32[]{:S(2)}) copy-start(f32[16,16]{0,1:T(8,128)} %constant.93.clone) | copy-start | bytes 3076
  0.0 13.2 %copy-start.7 = (f32[16,16]{0,1:T(8,128)S(1)}, f32[16,16]{0,1:T(8,128)}, u32[]{:S(2)}) copy-start(f32[16,16]{0,1:T(8,128)} %constant.94.clone) | copy-start | bytes 3076
  0.0 6.6 %copy-start.3 = (f32[16,32,128]{2,1,0:T(8,128)S(1)}, f32[16,32,128]{2,1,0:T(8,128)}, u32[]{:S(2)}) copy-start(f32[16,32,128]{2,1,0:T(8,128)} %param.10) | copy-start | bytes 786436
  0.0 13.0 %copy-start.8 = (f32[3,2,16]{2,1,0:T(2,128)S(1)}, f32[3,2,16]{2,1,0:T(2,128)}, u32[]{:S(2)}) copy-start(f32[3,2,16]{2,1,0:T(2,128)} %param.13) | copy-start | bytes 1156
  6.1 18.7 %collective-permute-start.2 = (f32[8,3,32,128]{3,2,1,0:T(8,128)}, f32[8,3,32,128]{3,2,1,0:T(8,128)S(1)}, u32[]{:S(2)}, u32[]{:S(2)}) collective-permute-start(f32[8,3,32,128]{3,2,1,0:T(8,128)} %get-tuple-element.14), channel_id=1, source_target_pairs={{0,1},{1,0},{2,3},{3,2},{4,5},{5,4},{6,7},{7,6},{8,9},{9,8},{10,11... | collective-permute-start | bytes 1179656 | tf_op jit(solution)/shard_map/ppermute | solution.py:464
  7.3 10.2 %collective-permute-start = (f32[16,6,128]{2,1,0:T(8,128)}, f32[16,6,128]{2,1,0:T(8,128)}, u32[]{:S(2)}, u32[]{:S(2)}) collective-permute-start(f32[16,6,128]{2,1,0:T(8,128)} %get-tuple-element.31), channel_id=1, source_target_pairs={{0,1},{1,2},{2,3},{3,4},{4,5},{5,6},{6,7},{7,8},{8,9},{9,10},{10,1... | collective-permute-start | bytes 147464 | tf_op jit(solution)/shard_map/ppermute | solution.py:427
  7.3 10.2 %collective-permute-start.1 = (f32[16,6,128]{2,1,0:T(8,128)}, f32[16,6,128]{2,1,0:T(8,128)}, u32[]{:S(2)}, u32[]{:S(2)}) collective-permute-start(f32[16,6,128]{2,1,0:T(8,128)} %get-tuple-element.32), channel_id=1, source_target_pairs={{0,15},{1,0},{2,1},{3,2},{4,3},{5,4},{6,5},{7,6},{8,7},{9,8},{10,9... | collective-permute-start | bytes 147464 | tf_op jit(solution)/shard_map/ppermute | solution.py:428
  13.4 6.8 %copy-start = (f32[6,528,128]{2,1,0:T(8,128)S(1)}, f32[6,528,128]{2,1,0:T(8,128)}, u32[]{:S(2)}) copy-start(f32[6,528,128]{2,1,0:T(8,128)} %constant.91.clone.table_hbm) | copy-start | bytes 4866052
  13.4 6.8 %copy-start.1 = (f32[3,128,128]{2,1,0:T(8,128)S(1)}, f32[3,128,128]{2,1,0:T(8,128)}, u32[]{:S(2)}) copy-start(f32[3,128,128]{2,1,0:T(8,128)} %blur_ref.1) | copy-start | bytes 589828
  13.5 6.8 %copy-start.2 = (f32[3,7]{1,0:T(4,128)S(1)}, f32[3,7]{1,0:T(4,128)}, u32[]{:S(2)}) copy-start(f32[3,7]{1,0:T(4,128)} %taps_ref.1) | copy-start | bytes 256
  20.2 4.6 %copy-start.5 = (f32[3,32,128]{2,1,0:T(8,128)S(1)}, f32[3,32,128]{2,1,0:T(8,128)}, u32[]{:S(2)}) copy-start(f32[3,32,128]{2,1,0:T(8,128)} %get-tuple-element.18) | copy-start | bytes 147460
  20.2 5.3 %copy-start.4 = (f32[1,3,32,128]{3,2,1,0:T(8,128)S(1)}, f32[1,3,32,128]{3,2,1,0:T(8,128)}, u32[]{:S(2)}) copy-start(f32[1,3,32,128]{3,2,1,0:T(8,128)} %get-tuple-element.19) | copy-start | bytes 147460
  24.9 13.3 %collective-permute-start.6 = (f32[2,3,32,128]{3,2,1,0:T(8,128)S(1)}, f32[2,3,32,128]{3,2,1,0:T(8,128)S(1)}, u32[]{:S(2)}, u32[]{:S(2)}) collective-permute-start(f32[2,3,32,128]{3,2,1,0:T(8,128)S(1)} %pad_maximum_fusion.4), channel_id=1, source_target_pairs={{0,8},{1,9},{2,10},{3,11},{4,12},{5,13},{6,14},{7,15},{8,0},{9,1},... | collective-permute-start | bytes 294920 | tf_op jit(solution)/shard_map/ppermute | solution.py:476
  25.6 12.6 %collective-permute-start.5 = (f32[2,3,32,128]{3,2,1,0:T(8,128)S(1)}, f32[2,3,32,128]{3,2,1,0:T(8,128)S(1)}, u32[]{:S(2)}, u32[]{:S(2)}) collective-permute-start(f32[2,3,32,128]{3,2,1,0:T(8,128)S(1)} %pad_maximum_fusion.3), channel_id=1, source_target_pairs={{0,6},{1,7},{2,4},{3,5},{4,2},{5,3},{6,0},{7,1},{8,14},{9,15},{10,... | collective-permute-start | bytes 294920 | tf_op jit(solution)/shard_map/ppermute | solution.py:476
  27.3 8.9 %collective-permute-start.4 = (f32[2,3,32,128]{3,2,1,0:T(8,128)S(1)}, f32[2,3,32,128]{3,2,1,0:T(8,128)S(1)}, u32[]{:S(2)}, u32[]{:S(2)}) collective-permute-start(f32[2,3,32,128]{3,2,1,0:T(8,128)S(1)} %pad_maximum_fusion.2), channel_id=1, source_target_pairs={{0,4},{1,5},{2,6},{3,7},{4,0},{5,1},{6,2},{7,3},{8,12},{9,13},{10,... | collective-permute-start | bytes 294920 | tf_op jit(solution)/shard_map/ppermute | solution.py:476
  27.8 6.6 %collective-permute-start.3 = (f32[2,3,32,128]{3,2,1,0:T(8,128)S(1)}, f32[2,3,32,128]{3,2,1,0:T(8,128)S(1)}, u32[]{:S(2)}, u32[]{:S(2)}) collective-permute-start(f32[2,3,32,128]{3,2,1,0:T(8,128)S(1)} %pad_maximum_fusion.1), channel_id=1, source_target_pairs={{0,2},{1,3},{2,0},{3,1},{4,6},{5,7},{6,4},{7,5},{8,10},{9,11},{10,... | collective-permute-start | bytes 294920 | tf_op jit(solution)/shard_map/ppermute | solution.py:476
  29.3 9.3 %collective-permute-start.7 = (f32[2,3,32,128]{3,2,1,0:T(8,128)S(1)}, f32[2,3,32,128]{3,2,1,0:T(8,128)S(1)}, u32[]{:S(2)}, u32[]{:S(2)}) collective-permute-start(f32[2,3,32,128]{3,2,1,0:T(8,128)S(1)} %pad_maximum_fusion.5), channel_id=1, source_target_pairs={{0,10},{1,11},{2,8},{3,9},{4,14},{5,15},{6,12},{7,13},{8,2},{9,3},... | collective-permute-start | bytes 294920 | tf_op jit(solution)/shard_map/ppermute | solution.py:476
  34.4 7.0 %collective-permute-start.8 = (f32[2,3,32,128]{3,2,1,0:T(8,128)S(1)}, f32[2,3,32,128]{3,2,1,0:T(8,128)S(1)}, u32[]{:S(2)}, u32[]{:S(2)}) collective-permute-start(f32[2,3,32,128]{3,2,1,0:T(8,128)S(1)} %pad_maximum_fusion.6), channel_id=1, source_target_pairs={{0,12},{1,13},{2,14},{3,15},{4,8},{5,9},{6,10},{7,11},{8,4},{9,5},... | collective-permute-start | bytes 294920 | tf_op jit(solution)/shard_map/ppermute | solution.py:476
  36.2 7.5 %collective-permute-start.9 = (f32[2,3,32,128]{3,2,1,0:T(8,128)S(1)}, f32[2,3,32,128]{3,2,1,0:T(8,128)S(1)}, u32[]{:S(2)}, u32[]{:S(2)}) collective-permute-start(f32[2,3,32,128]{3,2,1,0:T(8,128)S(1)} %pad_maximum_fusion.7), channel_id=1, source_target_pairs={{0,14},{1,15},{2,12},{3,13},{4,10},{5,11},{6,8},{7,9},{8,6},{9,7},... | collective-permute-start | bytes 294920 | tf_op jit(solution)/shard_map/ppermute | solution.py:476

commit v4 on v3

--- a/solution.py
+++ b/solution.py
@@ -281,7 +281,7 @@
     orients = table_ref.shape[0] // 2
     reach = (taps_ref.shape[1] - 1) // 2
     span = 2 * reach
-    step = max(d for d in range(1, 23) if out_ref.shape[0] % d == 0 and (d == 1 or d * planes <= 352))
+    step = max(d for d in range(1, 33) if out_ref.shape[0] % d == 0 and (d == 1 or d * planes <= 512))
 
     def lags_of(band, scale):
         return [
@@ -303,14 +303,13 @@
         return rows
 
     def weight_of(band):
-        matrix = blur_ref[band]
+        high, low = split(blur_ref[band])
         return weights(
             lax.dot_general(
-                matrix,
-                matrix,
+                jnp.concatenate([high, high, low], axis=0),
+                jnp.concatenate([high, low, high], axis=0),
                 (((0,), (0,)), ((), ())),
                 preferred_element_type=jnp.float32,
-                precision=lax.Precision.HIGHEST,
             )
         )
 
@@ -383,12 +382,14 @@
     width, planes, row_count = estimate_ref.shape
     depth = adjoint_ref.shape[1]
     high, low = split(adjoint_ref[...])
-    left_side = jnp.concatenate([high, high, low], axis=1)
+    left_side = jnp.concatenate(
+        [jnp.concatenate([high, high], axis=1), jnp.concatenate([low, low], axis=1)], axis=0
+    )
     for index in range(0, width, 2):
         columns = [received_ref[pl.ds(index + i, depth, stride=width), :] for i in range(2)]
         high, low = split(jnp.concatenate(columns, axis=1))
-        right_side = jnp.concatenate([high, low, high], axis=0)
-        product = wide_dot(left_side, right_side)
+        product = wide_dot(left_side, jnp.concatenate([high, low], axis=0))
+        product = product[:planes] + product[planes:]
         for i in range(2):
             out_ref[pl.ds(index + i, planes, stride=width), :] = (
                 estimate_ref[index + i] + product[:, i * row_count : (i + 1) * row_count]

time: 45.3 us -> 45 us (level)
  transfers between devices with their start and end apart: 10 -> 10, of which waited for: 4 -> 4; matrix products, arithmetic and copies ran while one was open for 17% -> 18% of each run, Pallas kernels for 10% -> 9%
where the time goes in v4:
time: 45 us; the launch traced here: 44.7 us
  starting transfers between devices  16.1 us (36%)
  Pallas kernels  11.6 us (26%)
  waiting for transfers between devices  8.72 us (19%)
  other arithmetic  2.95 us (7%)
  matrix products  2.71 us (6%)
  local copies, waits for them, and re-layouts  2.3 us (5%)
    ppermute x7, starting transfers between devices, exchange(): part = lax.ppermute(part, 'gz', [(s, s ^ 2 * bit) for s in range(ring)])  9.91 us
    ppermute x7, waiting for transfers between devices, exchange(): part = lax.ppermute(part, 'gz', [(s, s ^ 2 * bit) for s in range(ring)])  8.71 us
    pallas_call x1, Pallas kernels, data_sums(): pl.pallas_call(data_kernel, out_shape=[jax.ShapeDtypeStruct((chunks // co...  6.05 us
    ppermute x1, starting transfers between devices, halo(): rights.append(lax.ppermute(estimate[:, :take], 'gz', back))  5.64 us
    pallas_call x1, Pallas kernels, estimate_part(): pl.pallas_call(estimate_kernel, out_shape=jax.ShapeDtypeStruct((width, pl...  4.17 us
    neg x1, other arithmetic, exchange(): own = -lax.dynamic_index_in_dim(mine, chip ^ bit, 0, keepdims=False)  1.77 us
    dot_general x1, matrix products, exact_dot(): jnp.dot(left_side, right_side, preferred_element_type=jnp.float32, precis...  1.72 us
    pallas_call x1, Pallas kernels, combine(): pl.pallas_call(combine_kernel, out_shape=jax.ShapeDtypeStruct((planes * w...  1.34 us
  transfers between devices with their start and end apart: 10, of which 4 were waited for; matrix products, arithmetic and copies ran while one was open for 18% of the time, Pallas kernels for 9%

profile of v4, /device:TPU:0, one launch (start us, length us, event | category | flops | bytes accessed | tf_op | source)
XLA Modules:
  0.0 44.7 jit_solution(17801433659497288717)
XLA Ops:
  0.0 0.0 copy-start.6
  0.0 6.0 %data_sums.1 = (f32[8,3,32,128]{3,2,1,0:T(8,128)}, f32[8,3,32,128]{3,2,1,0:T(8,128)}) custom-call(s32[3,5]{1,0:T(4,128)} %phase_hbm.1, f32[3,7]{1,0:T(4,128)} %taps_ref.1, s32[3,5,1,512,128]{4,3,2,1,0:T(8,128)} %frames_hbm.1, f32[3,128,128]{2,1,0:T(8,128)} %blur_ref.1, f32[6,528,128]{2,1,0:T(8,128)} %constant.91.clone.table_hbm), custom_call_target="tpu_custom_call" | custom-call | flops 872415232 | bytes 3932160 | tf_op jit(solution)/shard_map/data_sums/pallas_call | solution.py:242
  6.1 0.6 %collective-permute-start.2 = (f32[8,3,32,128]{3,2,1,0:T(8,128)}, f32[8,3,32,128]{3,2,1,0:T(8,128)S(1)}, u32[]{:S(2)}, u32[]{:S(2)}) collective-permute-start(f32[8,3,32,128]{3,2,1,0:T(8,128)} %get-tuple-element.14), channel_id=1, source_target_pairs={{0,1},{1,0},{2,3},{3,2},{4,5},{5,4},{6,7},{7,6},{8,9},{9,8},{10,11... | collective-permute-start | bytes 1179656 | tf_op jit(solution)/shard_map/ppermute | solution.py:465
  6.6 0.0 copy-done.3
  6.6 0.7 %fusion.20 = (f32[16,6,128]{2,1,0:T(8,128)}, f32[16,6,128]{2,1,0:T(8,128)}) fusion(f32[16,32,128]{2,1,0:T(8,128)S(1)} %copy-done.3), kind=kLoop, calls=%fused_computation.64 | loop fusion | bytes 196608 | tf_op jit(solution)/shard_map/slice | solution.py:428
  7.3 0.0 collective-permute-start
  7.3 5.6 %collective-permute-start.1 = (f32[16,6,128]{2,1,0:T(8,128)}, f32[16,6,128]{2,1,0:T(8,128)}, u32[]{:S(2)}, u32[]{:S(2)}) collective-permute-start(f32[16,6,128]{2,1,0:T(8,128)} %get-tuple-element.32), channel_id=1, source_target_pairs={{0,15},{1,0},{2,1},{3,2},{4,3},{5,4},{6,5},{7,6},{8,7},{9,8},{10,9... | collective-permute-start | bytes 147464 | tf_op jit(solution)/shard_map/ppermute | solution.py:429
  13.0 0.0 copy-done.8
  13.0 0.1 fusion.17
  13.2 0.0 copy-done.6
  13.2 0.0 copy-done.7
  13.2 0.2 fusion.1
  13.4 0.0 copy-start
  13.4 0.0 copy-start.1
  13.5 0.0 copy-start.2
  13.5 1.8 %dynamic-slice_negate_fusion.1 = (f32[1,3,32,128]{3,2,1,0:T(8,128)S(1)}, f32[1,3,32,128]{3,2,1,0:T(8,128)S(1)}, f32[1,3,32,128]{3,2,1,0:T(8,128)S(1)}, f32[3,32,...) fusion(f32[8,3,32,128]{3,2,1,0:T(8,128)} %get-tuple-element.13,, ...), kind=kLoop, calls=%fused_computation.14 | loop fusion | flops 98303 | bytes 786464 | tf_op jit(solution)/shard_map/neg | solution.py:473
  15.2 0.8 %convolution_bitcast_fusion.1 = f32[3,16,16,1]{2,1,3,0:T(8,128)} fusion(f32[3,16,16]{2,1,0:T(8,128)S(1)} %fusion.1), kind=kOutput, calls=%fused_computation.1 | convolution fusion | flops 147456 | bytes 6144 | tf_op jit(solution)/shard_map/mzw,mzv->mwv/dot_general | solution.py:498
  16.0 0.7 %copy.12 = f32[16,16,3]{0,2,1:T(4,128)} copy(f32[16,16,3]{1,0,2:T(8,128)S(1)} %bitcast.42) | data formatting | bytes 6144 | tf_op jit(solution)/shard_map/transpose;zk,mkw->mzw/transpose | solution.py:402
  16.7 0.8 %reshape.26 = f32[16,48]{0,1:T(8,128)S(1)} reshape(f32[16,16,3]{0,2,1:T(4,128)} %copy.12) | data formatting | bytes 6144 | tf_op jit(solution)/shard_map/reshape | solution.py:402
  17.5 0.1 copy.14.adjoint_ref
  17.5 0.0 collective-permute-done
  17.5 0.0 collective-permute-done.1
  17.5 0.9 %pad_maximum_fusion = f32[16,44,128]{2,1,0:T(8,128)S(1)} fusion(f32[16,6,128]{2,1,0:T(8,128)} %collective-permute-done.1, f32[16,32,128]{2,1,0:T(8,128)S(1)} %copy-done.3, f32[16,6,128]{2,1,0:T(8,128)} %collective-permute-done), kind=kLoop, calls=%fused_computation.2 | loop fusion | flops 180224 | bytes 720896 | tf_op jit(solution)/shard_map/concatenate | solution.py:499
  18.5 1.7 %convolution_bitcast_fusion.axial_ref = f32[3,44,16,128]{3,2,1,0:T(8,128)S(1)} fusion(f32[3,16,16,1]{2,1,3,0:T(8,128)} %convolution_bitcast_fusion.1, f32[2,8,44,128]{3,2,1,0:T(8,128)S(1)} %bitcast.41), kind=kOutput, calls=%fused_computation | convolution fusion | flops 51904512 | bytes 1444864 | tf_op jit(solution)/shard_map/dot_general | solution.py:19
  20.2 0.0 copy-done
  20.2 0.0 copy-done.1
  20.2 0.0 copy-done.2
  20.2 0.0 copy-start.5
  20.2 0.0 copy-start.4
  20.3 4.2 %estimate_part.1.estimate_ref = f32[32,16,128]{2,1,0:T(8,128)S(1)} custom-call(f32[3,7]{1,0:T(4,128)S(1)} %copy-done.2, f32[3,44,16,128]{3,2,1,0:T(8,128)S(1)} %convolution_bitcast_fusion.axial_ref, f32[6,528,128]{2,1,0:T(8,128)S(1)} %copy-done, f32[3,128,128]{2,1,0:T(8,128)S(1)} %copy-done.1), custom_call_target="tpu_custom_call" | custom-call | flops 16106127360 | bytes 1081344 | tf_op jit(solution)/shard_map/estimate_part/pallas_call | solution.py:367
  24.4 0.0 collective-permute-done.2
  24.5 0.0 copy-done.5
  24.5 0.6 %collective-permute-start.6 = (f32[2,3,32,128]{3,2,1,0:T(8,128)S(1)}, f32[2,3,32,128]{3,2,1,0:T(8,128)S(1)}, u32[]{:S(2)}, u32[]{:S(2)}) collective-permute-start(f32[2,3,32,128]{3,2,1,0:T(8,128)S(1)} %pad_maximum_fusion.4), channel_id=1, source_target_pairs={{0,8},{1,9},{2,10},{3,11},{4,12},{5,13},{6,14},{7,15},{8,0},{9,1},... | collective-permute-start | bytes 294920 | tf_op jit(solution)/shard_map/ppermute | solution.py:477
  25.2 0.0 copy-done.4
  25.2 1.7 %collective-permute-start.5 = (f32[2,3,32,128]{3,2,1,0:T(8,128)S(1)}, f32[2,3,32,128]{3,2,1,0:T(8,128)S(1)}, u32[]{:S(2)}, u32[]{:S(2)}) collective-permute-start(f32[2,3,32,128]{3,2,1,0:T(8,128)S(1)} %pad_maximum_fusion.3), channel_id=1, source_target_pairs={{0,6},{1,7},{2,4},{3,5},{4,2},{5,3},{6,0},{7,1},{8,14},{9,15},{10,... | collective-permute-start | bytes 294920 | tf_op jit(solution)/shard_map/ppermute | solution.py:477
  26.9 0.5 %collective-permute-start.4 = (f32[2,3,32,128]{3,2,1,0:T(8,128)S(1)}, f32[2,3,32,128]{3,2,1,0:T(8,128)S(1)}, u32[]{:S(2)}, u32[]{:S(2)}) collective-permute-start(f32[2,3,32,128]{3,2,1,0:T(8,128)S(1)} %pad_maximum_fusion.2), channel_id=1, source_target_pairs={{0,4},{1,5},{2,6},{3,7},{4,0},{5,1},{6,2},{7,3},{8,12},{9,13},{10,... | collective-permute-start | bytes 294920 | tf_op jit(solution)/shard_map/ppermute | solution.py:477
  27.4 1.5 %collective-permute-start.3 = (f32[2,3,32,128]{3,2,1,0:T(8,128)S(1)}, f32[2,3,32,128]{3,2,1,0:T(8,128)S(1)}, u32[]{:S(2)}, u32[]{:S(2)}) collective-permute-start(f32[2,3,32,128]{3,2,1,0:T(8,128)S(1)} %pad_maximum_fusion.1), channel_id=1, source_target_pairs={{0,2},{1,3},{2,0},{3,1},{4,6},{5,7},{6,4},{7,5},{8,10},{9,11},{10,... | collective-permute-start | bytes 294920 | tf_op jit(solution)/shard_map/ppermute | solution.py:477
  28.9 1.9 %collective-permute-start.7 = (f32[2,3,32,128]{3,2,1,0:T(8,128)S(1)}, f32[2,3,32,128]{3,2,1,0:T(8,128)S(1)}, u32[]{:S(2)}, u32[]{:S(2)}) collective-permute-start(f32[2,3,32,128]{3,2,1,0:T(8,128)S(1)} %pad_maximum_fusion.5), channel_id=1, source_target_pairs={{0,10},{1,11},{2,8},{3,9},{4,14},{5,15},{6,12},{7,13},{8,2},{9,3},... | collective-permute-start | bytes 294920 | tf_op jit(solution)/shard_map/ppermute | solution.py:477
  30.8 3.3 %collective-permute-done.3 = f32[2,3,32,128]{3,2,1,0:T(8,128)S(1)} collective-permute-done((f32[2,3,32,128]{3,2,1,0:T(8,128)S(1)}, f32[2,3,32,128]{3,2,1,0:T(8,128)S(1)}, u32[]{:S(2)}, u32[]{:S(2)}) %collective-permute-start.3) | collective-permute-done | bytes 98336 | tf_op jit(solution)/shard_map/ppermute | solution.py:477
  34.0 1.8 %collective-permute-start.8 = (f32[2,3,32,128]{3,2,1,0:T(8,128)S(1)}, f32[2,3,32,128]{3,2,1,0:T(8,128)S(1)}, u32[]{:S(2)}, u32[]{:S(2)}) collective-permute-start(f32[2,3,32,128]{3,2,1,0:T(8,128)S(1)} %pad_maximum_fusion.6), channel_id=1, source_target_pairs={{0,12},{1,13},{2,14},{3,15},{4,8},{5,9},{6,10},{7,11},{8,4},{9,5},... | collective-permute-start | bytes 294920 | tf_op jit(solution)/shard_map/ppermute | solution.py:477
  35.8 0.0 collective-permute-done.4
  35.8 2.0 %collective-permute-start.9 = (f32[2,3,32,128]{3,2,1,0:T(8,128)S(1)}, f32[2,3,32,128]{3,2,1,0:T(8,128)S(1)}, u32[]{:S(2)}, u32[]{:S(2)}) collective-permute-start(f32[2,3,32,128]{3,2,1,0:T(8,128)S(1)} %pad_maximum_fusion.7), channel_id=1, source_target_pairs={{0,14},{1,15},{2,12},{3,13},{4,10},{5,11},{6,8},{7,9},{8,6},{9,7},... | collective-permute-start | bytes 294920 | tf_op jit(solution)/shard_map/ppermute | solution.py:477
  37.8 0.0 collective-permute-done.5
  37.8 0.0 collective-permute-done.6
  37.9 0.3 collective-permute-done.7
  38.2 2.9 %collective-permute-done.8 = f32[2,3,32,128]{3,2,1,0:T(8,128)S(1)} collective-permute-done((f32[2,3,32,128]{3,2,1,0:T(8,128)S(1)}, f32[2,3,32,128]{3,2,1,0:T(8,128)S(1)}, u32[]{:S(2)}, u32[]{:S(2)}) %collective-permute-start.8) | collective-permute-done | bytes 98336 | tf_op jit(solution)/shard_map/ppermute | solution.py:477
  41.1 2.3 %collective-permute-done.9 = f32[2,3,32,128]{3,2,1,0:T(8,128)S(1)} collective-permute-done((f32[2,3,32,128]{3,2,1,0:T(8,128)S(1)}, f32[2,3,32,128]{3,2,1,0:T(8,128)S(1)}, u32[]{:S(2)}, u32[]{:S(2)}) %collective-permute-start.9) | collective-permute-done | bytes 98336 | tf_op jit(solution)/shard_map/ppermute | solution.py:477
  43.3 1.3 %combine.1 = f32[512,128]{1,0:T(8,128)} custom-call(f32[16,48]{1,0:T(8,128)S(1)} %copy.14.adjoint_ref, f32[32,16,128]{2,1,0:T(8,128)S(1)} %estimate_part.1.estimate_ref, f32[1536,128]{1,0:T(8,128)S(1)} %bitcast.40), custom_call_target="tpu_custom_call" | custom-call | flops 6291456 | bytes 786432 | tf_op jit(solution)/shard_map/combine/pallas_call | solution.py:404
  (22 shorter events, 0.2 us)
Async XLA Ops:
  0.0 13.2 %copy-start.6 = (f32[16,16]{0,1:T(8,128)S(1)}, f32[16,16]{0,1:T(8,128)}, u32[]{:S(2)}) copy-start(f32[16,16]{0,1:T(8,128)} %constant.93.clone) | copy-start | bytes 3076
  0.0 13.2 %copy-start.7 = (f32[16,16]{0,1:T(8,128)S(1)}, f32[16,16]{0,1:T(8,128)}, u32[]{:S(2)}) copy-start(f32[16,16]{0,1:T(8,128)} %constant.94.clone) | copy-start | bytes 3076
  0.0 6.6 %copy-start.3 = (f32[16,32,128]{2,1,0:T(8,128)S(1)}, f32[16,32,128]{2,1,0:T(8,128)}, u32[]{:S(2)}) copy-start(f32[16,32,128]{2,1,0:T(8,128)} %param.10) | copy-start | bytes 786436
  0.0 13.0 %copy-start.8 = (f32[3,2,16]{2,1,0:T(2,128)S(1)}, f32[3,2,16]{2,1,0:T(2,128)}, u32[]{:S(2)}) copy-start(f32[3,2,16]{2,1,0:T(2,128)} %param.13) | copy-start | bytes 1156
  6.1 18.4 %collective-permute-start.2 = (f32[8,3,32,128]{3,2,1,0:T(8,128)}, f32[8,3,32,128]{3,2,1,0:T(8,128)S(1)}, u32[]{:S(2)}, u32[]{:S(2)}) collective-permute-start(f32[8,3,32,128]{3,2,1,0:T(8,128)} %get-tuple-element.14), channel_id=1, source_target_pairs={{0,1},{1,0},{2,3},{3,2},{4,5},{5,4},{6,7},{7,6},{8,9},{9,8},{10,11... | collective-permute-start | bytes 1179656 | tf_op jit(solution)/shard_map/ppermute | solution.py:465
  7.3 10.2 %collective-permute-start = (f32[16,6,128]{2,1,0:T(8,128)}, f32[16,6,128]{2,1,0:T(8,128)}, u32[]{:S(2)}, u32[]{:S(2)}) collective-permute-start(f32[16,6,128]{2,1,0:T(8,128)} %get-tuple-element.31), channel_id=1, source_target_pairs={{0,1},{1,2},{2,3},{3,4},{4,5},{5,6},{6,7},{7,8},{8,9},{9,10},{10,1... | collective-permute-start | bytes 147464 | tf_op jit(solution)/shard_map/ppermute | solution.py:428
  7.3 10.2 %collective-permute-start.1 = (f32[16,6,128]{2,1,0:T(8,128)}, f32[16,6,128]{2,1,0:T(8,128)}, u32[]{:S(2)}, u32[]{:S(2)}) collective-permute-start(f32[16,6,128]{2,1,0:T(8,128)} %get-tuple-element.32), channel_id=1, source_target_pairs={{0,15},{1,0},{2,1},{3,2},{4,3},{5,4},{6,5},{7,6},{8,7},{9,8},{10,9... | collective-permute-start | bytes 147464 | tf_op jit(solution)/shard_map/ppermute | solution.py:429
  13.4 6.8 %copy-start = (f32[6,528,128]{2,1,0:T(8,128)S(1)}, f32[6,528,128]{2,1,0:T(8,128)}, u32[]{:S(2)}) copy-start(f32[6,528,128]{2,1,0:T(8,128)} %constant.91.clone.table_hbm) | copy-start | bytes 4866052
  13.4 6.8 %copy-start.1 = (f32[3,128,128]{2,1,0:T(8,128)S(1)}, f32[3,128,128]{2,1,0:T(8,128)}, u32[]{:S(2)}) copy-start(f32[3,128,128]{2,1,0:T(8,128)} %blur_ref.1) | copy-start | bytes 589828
  13.5 6.8 %copy-start.2 = (f32[3,7]{1,0:T(4,128)S(1)}, f32[3,7]{1,0:T(4,128)}, u32[]{:S(2)}) copy-start(f32[3,7]{1,0:T(4,128)} %taps_ref.1) | copy-start | bytes 256
  20.2 4.3 %copy-start.5 = (f32[3,32,128]{2,1,0:T(8,128)S(1)}, f32[3,32,128]{2,1,0:T(8,128)}, u32[]{:S(2)}) copy-start(f32[3,32,128]{2,1,0:T(8,128)} %get-tuple-element.18) | copy-start | bytes 147460
  20.2 4.9 %copy-start.4 = (f32[1,3,32,128]{3,2,1,0:T(8,128)S(1)}, f32[1,3,32,128]{3,2,1,0:T(8,128)}, u32[]{:S(2)}) copy-start(f32[1,3,32,128]{3,2,1,0:T(8,128)} %get-tuple-element.19) | copy-start | bytes 147460
  24.5 13.3 %collective-permute-start.6 = (f32[2,3,32,128]{3,2,1,0:T(8,128)S(1)}, f32[2,3,32,128]{3,2,1,0:T(8,128)S(1)}, u32[]{:S(2)}, u32[]{:S(2)}) collective-permute-start(f32[2,3,32,128]{3,2,1,0:T(8,128)S(1)} %pad_maximum_fusion.4), channel_id=1, source_target_pairs={{0,8},{1,9},{2,10},{3,11},{4,12},{5,13},{6,14},{7,15},{8,0},{9,1},... | collective-permute-start | bytes 294920 | tf_op jit(solution)/shard_map/ppermute | solution.py:477
  25.2 12.6 %collective-permute-start.5 = (f32[2,3,32,128]{3,2,1,0:T(8,128)S(1)}, f32[2,3,32,128]{3,2,1,0:T(8,128)S(1)}, u32[]{:S(2)}, u32[]{:S(2)}) collective-permute-start(f32[2,3,32,128]{3,2,1,0:T(8,128)S(1)} %pad_maximum_fusion.3), channel_id=1, source_target_pairs={{0,6},{1,7},{2,4},{3,5},{4,2},{5,3},{6,0},{7,1},{8,14},{9,15},{10,... | collective-permute-start | bytes 294920 | tf_op jit(solution)/shard_map/ppermute | solution.py:477
  26.9 8.9 %collective-permute-start.4 = (f32[2,3,32,128]{3,2,1,0:T(8,128)S(1)}, f32[2,3,32,128]{3,2,1,0:T(8,128)S(1)}, u32[]{:S(2)}, u32[]{:S(2)}) collective-permute-start(f32[2,3,32,128]{3,2,1,0:T(8,128)S(1)} %pad_maximum_fusion.2), channel_id=1, source_target_pairs={{0,4},{1,5},{2,6},{3,7},{4,0},{5,1},{6,2},{7,3},{8,12},{9,13},{10,... | collective-permute-start | bytes 294920 | tf_op jit(solution)/shard_map/ppermute | solution.py:477
  27.4 6.6 %collective-permute-start.3 = (f32[2,3,32,128]{3,2,1,0:T(8,128)S(1)}, f32[2,3,32,128]{3,2,1,0:T(8,128)S(1)}, u32[]{:S(2)}, u32[]{:S(2)}) collective-permute-start(f32[2,3,32,128]{3,2,1,0:T(8,128)S(1)} %pad_maximum_fusion.1), channel_id=1, source_target_pairs={{0,2},{1,3},{2,0},{3,1},{4,6},{5,7},{6,4},{7,5},{8,10},{9,11},{10,... | collective-permute-start | bytes 294920 | tf_op jit(solution)/shard_map/ppermute | solution.py:477
  28.9 9.3 %collective-permute-start.7 = (f32[2,3,32,128]{3,2,1,0:T(8,128)S(1)}, f32[2,3,32,128]{3,2,1,0:T(8,128)S(1)}, u32[]{:S(2)}, u32[]{:S(2)}) collective-permute-start(f32[2,3,32,128]{3,2,1,0:T(8,128)S(1)} %pad_maximum_fusion.5), channel_id=1, source_target_pairs={{0,10},{1,11},{2,8},{3,9},{4,14},{5,15},{6,12},{7,13},{8,2},{9,3},... | collective-permute-start | bytes 294920 | tf_op jit(solution)/shard_map/ppermute | solution.py:477
  34.0 7.0 %collective-permute-start.8 = (f32[2,3,32,128]{3,2,1,0:T(8,128)S(1)}, f32[2,3,32,128]{3,2,1,0:T(8,128)S(1)}, u32[]{:S(2)}, u32[]{:S(2)}) collective-permute-start(f32[2,3,32,128]{3,2,1,0:T(8,128)S(1)} %pad_maximum_fusion.6), channel_id=1, source_target_pairs={{0,12},{1,13},{2,14},{3,15},{4,8},{5,9},{6,10},{7,11},{8,4},{9,5},... | collective-permute-start | bytes 294920 | tf_op jit(solution)/shard_map/ppermute | solution.py:477
  35.8 7.5 %collective-permute-start.9 = (f32[2,3,32,128]{3,2,1,0:T(8,128)S(1)}, f32[2,3,32,128]{3,2,1,0:T(8,128)S(1)}, u32[]{:S(2)}, u32[]{:S(2)}) collective-permute-start(f32[2,3,32,128]{3,2,1,0:T(8,128)S(1)} %pad_maximum_fusion.7), channel_id=1, source_target_pairs={{0,14},{1,15},{2,12},{3,13},{4,10},{5,11},{6,8},{7,9},{8,6},{9,7},... | collective-permute-start | bytes 294920 | tf_op jit(solution)/shard_map/ppermute | solution.py:477

commit v5 on v4

--- a/solution.py
+++ b/solution.py
@@ -382,14 +382,12 @@
     width, planes, row_count = estimate_ref.shape
     depth = adjoint_ref.shape[1]
     high, low = split(adjoint_ref[...])
-    left_side = jnp.concatenate(
-        [jnp.concatenate([high, high], axis=1), jnp.concatenate([low, low], axis=1)], axis=0
-    )
+    left_side = jnp.concatenate([high, high, low], axis=1)
     for index in range(0, width, 2):
         columns = [received_ref[pl.ds(index + i, depth, stride=width), :] for i in range(2)]
         high, low = split(jnp.concatenate(columns, axis=1))
-        product = wide_dot(left_side, jnp.concatenate([high, low], axis=0))
-        product = product[:planes] + product[planes:]
+        right_side = jnp.concatenate([high, low, high], axis=0)
+        product = wide_dot(left_side, right_side)
         for i in range(2):
             out_ref[pl.ds(index + i, planes, stride=width), :] = (
                 estimate_ref[index + i] + product[:, i * row_count : (i + 1) * row_count]

time: 45 us -> 45 us (level)
  no operation moved by 1% of the time
where the time goes in v5:
time: 45 us; the launch traced here: 44.6 us
  starting transfers between devices  16.1 us (36%)
  Pallas kernels  11.5 us (26%)
  waiting for transfers between devices  8.72 us (19%)
  other arithmetic  2.95 us (7%)
  matrix products  2.71 us (6%)
  local copies, waits for them, and re-layouts  2.3 us (5%)
    ppermute x7, starting transfers between devices, exchange(): part = lax.ppermute(part, 'gz', [(s, s ^ 2 * bit) for s in range(ring)])  9.91 us
    ppermute x7, waiting for transfers between devices, exchange(): part = lax.ppermute(part, 'gz', [(s, s ^ 2 * bit) for s in range(ring)])  8.71 us
    pallas_call x1, Pallas kernels, data_sums(): pl.pallas_call(data_kernel, out_shape=[jax.ShapeDtypeStruct((chunks // co...  6.05 us
    ppermute x1, starting transfers between devices, halo(): rights.append(lax.ppermute(estimate[:, :take], 'gz', back))  5.64 us
    pallas_call x1, Pallas kernels, estimate_part(): pl.pallas_call(estimate_kernel, out_shape=jax.ShapeDtypeStruct((width, pl...  4.17 us
    neg x1, other arithmetic, exchange(): own = -lax.dynamic_index_in_dim(mine, chip ^ bit, 0, keepdims=False)  1.77 us
    dot_general x1, matrix products, exact_dot(): jnp.dot(left_side, right_side, preferred_element_type=jnp.float32, precis...  1.72 us
    pallas_call x1, Pallas kernels, combine(): pl.pallas_call(combine_kernel, out_shape=jax.ShapeDtypeStruct((planes * w...  1.32 us
  transfers between devices with their start and end apart: 10, of which 4 were waited for; matrix products, arithmetic and copies ran while one was open for 18% of the time, Pallas kernels for 9%

profile of v5, /device:TPU:0, one launch (start us, length us, event | category | flops | bytes accessed | tf_op | source)
XLA Modules:
  0.0 44.6 jit_solution(15421139051534952771)
XLA Ops:
  0.0 0.0 copy-start.6
  0.0 6.0 %data_sums.1 = (f32[8,3,32,128]{3,2,1,0:T(8,128)}, f32[8,3,32,128]{3,2,1,0:T(8,128)}) custom-call(s32[3,5]{1,0:T(4,128)} %phase_hbm.1, f32[3,7]{1,0:T(4,128)} %taps_ref.1, s32[3,5,1,512,128]{4,3,2,1,0:T(8,128)} %frames_hbm.1, f32[3,128,128]{2,1,0:T(8,128)} %blur_ref.1, f32[6,528,128]{2,1,0:T(8,128)} %constant.91.clone.table_hbm), custom_call_target="tpu_custom_call" | custom-call | flops 872415232 | bytes 3932160 | tf_op jit(solution)/shard_map/data_sums/pallas_call | solution.py:242
  6.1 0.6 %collective-permute-start.2 = (f32[8,3,32,128]{3,2,1,0:T(8,128)}, f32[8,3,32,128]{3,2,1,0:T(8,128)S(1)}, u32[]{:S(2)}, u32[]{:S(2)}) collective-permute-start(f32[8,3,32,128]{3,2,1,0:T(8,128)} %get-tuple-element.14), channel_id=1, source_target_pairs={{0,1},{1,0},{2,3},{3,2},{4,5},{5,4},{6,7},{7,6},{8,9},{9,8},{10,11... | collective-permute-start | bytes 1179656 | tf_op jit(solution)/shard_map/ppermute | solution.py:463
  6.6 0.0 copy-done.3
  6.6 0.7 %fusion.20 = (f32[16,6,128]{2,1,0:T(8,128)}, f32[16,6,128]{2,1,0:T(8,128)}) fusion(f32[16,32,128]{2,1,0:T(8,128)S(1)} %copy-done.3), kind=kLoop, calls=%fused_computation.64 | loop fusion | bytes 196608 | tf_op jit(solution)/shard_map/slice | solution.py:426
  7.3 0.0 collective-permute-start
  7.3 5.6 %collective-permute-start.1 = (f32[16,6,128]{2,1,0:T(8,128)}, f32[16,6,128]{2,1,0:T(8,128)}, u32[]{:S(2)}, u32[]{:S(2)}) collective-permute-start(f32[16,6,128]{2,1,0:T(8,128)} %get-tuple-element.32), channel_id=1, source_target_pairs={{0,15},{1,0},{2,1},{3,2},{4,3},{5,4},{6,5},{7,6},{8,7},{9,8},{10,9... | collective-permute-start | bytes 147464 | tf_op jit(solution)/shard_map/ppermute | solution.py:427
  13.0 0.0 copy-done.8
  13.0 0.1 fusion.17
  13.2 0.0 copy-done.6
  13.2 0.0 copy-done.7
  13.2 0.2 fusion.1
  13.4 0.0 copy-start
  13.4 0.0 copy-start.1
  13.5 0.0 copy-start.2
  13.5 1.8 %dynamic-slice_negate_fusion.1 = (f32[1,3,32,128]{3,2,1,0:T(8,128)S(1)}, f32[1,3,32,128]{3,2,1,0:T(8,128)S(1)}, f32[1,3,32,128]{3,2,1,0:T(8,128)S(1)}, f32[3,32,...) fusion(f32[8,3,32,128]{3,2,1,0:T(8,128)} %get-tuple-element.13,, ...), kind=kLoop, calls=%fused_computation.14 | loop fusion | flops 98303 | bytes 786464 | tf_op jit(solution)/shard_map/neg | solution.py:471
  15.2 0.8 %convolution_bitcast_fusion.1 = f32[3,16,16,1]{2,1,3,0:T(8,128)} fusion(f32[3,16,16]{2,1,0:T(8,128)S(1)} %fusion.1), kind=kOutput, calls=%fused_computation.1 | convolution fusion | flops 147456 | bytes 6144 | tf_op jit(solution)/shard_map/mzw,mzv->mwv/dot_general | solution.py:496
  16.0 0.7 %copy.12 = f32[16,16,3]{0,2,1:T(4,128)} copy(f32[16,16,3]{1,0,2:T(8,128)S(1)} %bitcast.42) | data formatting | bytes 6144 | tf_op jit(solution)/shard_map/transpose;zk,mkw->mzw/transpose | solution.py:400
  16.7 0.8 %reshape.26 = f32[16,48]{0,1:T(8,128)S(1)} reshape(f32[16,16,3]{0,2,1:T(4,128)} %copy.12) | data formatting | bytes 6144 | tf_op jit(solution)/shard_map/reshape | solution.py:400
  17.5 0.1 copy.14.adjoint_ref
  17.5 0.0 collective-permute-done
  17.5 0.0 collective-permute-done.1
  17.5 0.9 %pad_maximum_fusion = f32[16,44,128]{2,1,0:T(8,128)S(1)} fusion(f32[16,6,128]{2,1,0:T(8,128)} %collective-permute-done.1, f32[16,32,128]{2,1,0:T(8,128)S(1)} %copy-done.3, f32[16,6,128]{2,1,0:T(8,128)} %collective-permute-done), kind=kLoop, calls=%fused_computation.2 | loop fusion | flops 180224 | bytes 720896 | tf_op jit(solution)/shard_map/concatenate | solution.py:497
  18.5 1.7 %convolution_bitcast_fusion.axial_ref = f32[3,44,16,128]{3,2,1,0:T(8,128)S(1)} fusion(f32[3,16,16,1]{2,1,3,0:T(8,128)} %convolution_bitcast_fusion.1, f32[2,8,44,128]{3,2,1,0:T(8,128)S(1)} %bitcast.41), kind=kOutput, calls=%fused_computation | convolution fusion | flops 51904512 | bytes 1444864 | tf_op jit(solution)/shard_map/dot_general | solution.py:19
  20.2 0.0 copy-done
  20.2 0.0 copy-done.1
  20.2 0.0 copy-done.2
  20.2 0.0 copy-start.5
  20.2 0.0 copy-start.4
  20.3 4.2 %estimate_part.1.estimate_ref = f32[32,16,128]{2,1,0:T(8,128)S(1)} custom-call(f32[3,7]{1,0:T(4,128)S(1)} %copy-done.2, f32[3,44,16,128]{3,2,1,0:T(8,128)S(1)} %convolution_bitcast_fusion.axial_ref, f32[6,528,128]{2,1,0:T(8,128)S(1)} %copy-done, f32[3,128,128]{2,1,0:T(8,128)S(1)} %copy-done.1), custom_call_target="tpu_custom_call" | custom-call | flops 16106127360 | bytes 1081344 | tf_op jit(solution)/shard_map/estimate_part/pallas_call | solution.py:367
  24.4 0.0 collective-permute-done.2
  24.5 0.0 copy-done.5
  24.5 0.6 %collective-permute-start.6 = (f32[2,3,32,128]{3,2,1,0:T(8,128)S(1)}, f32[2,3,32,128]{3,2,1,0:T(8,128)S(1)}, u32[]{:S(2)}, u32[]{:S(2)}) collective-permute-start(f32[2,3,32,128]{3,2,1,0:T(8,128)S(1)} %pad_maximum_fusion.4), channel_id=1, source_target_pairs={{0,8},{1,9},{2,10},{3,11},{4,12},{5,13},{6,14},{7,15},{8,0},{9,1},... | collective-permute-start | bytes 294920 | tf_op jit(solution)/shard_map/ppermute | solution.py:475
  25.2 0.0 copy-done.4
  25.2 1.7 %collective-permute-start.5 = (f32[2,3,32,128]{3,2,1,0:T(8,128)S(1)}, f32[2,3,32,128]{3,2,1,0:T(8,128)S(1)}, u32[]{:S(2)}, u32[]{:S(2)}) collective-permute-start(f32[2,3,32,128]{3,2,1,0:T(8,128)S(1)} %pad_maximum_fusion.3), channel_id=1, source_target_pairs={{0,6},{1,7},{2,4},{3,5},{4,2},{5,3},{6,0},{7,1},{8,14},{9,15},{10,... | collective-permute-start | bytes 294920 | tf_op jit(solution)/shard_map/ppermute | solution.py:475
  26.9 0.5 %collective-permute-start.4 = (f32[2,3,32,128]{3,2,1,0:T(8,128)S(1)}, f32[2,3,32,128]{3,2,1,0:T(8,128)S(1)}, u32[]{:S(2)}, u32[]{:S(2)}) collective-permute-start(f32[2,3,32,128]{3,2,1,0:T(8,128)S(1)} %pad_maximum_fusion.2), channel_id=1, source_target_pairs={{0,4},{1,5},{2,6},{3,7},{4,0},{5,1},{6,2},{7,3},{8,12},{9,13},{10,... | collective-permute-start | bytes 294920 | tf_op jit(solution)/shard_map/ppermute | solution.py:475
  27.4 1.5 %collective-permute-start.3 = (f32[2,3,32,128]{3,2,1,0:T(8,128)S(1)}, f32[2,3,32,128]{3,2,1,0:T(8,128)S(1)}, u32[]{:S(2)}, u32[]{:S(2)}) collective-permute-start(f32[2,3,32,128]{3,2,1,0:T(8,128)S(1)} %pad_maximum_fusion.1), channel_id=1, source_target_pairs={{0,2},{1,3},{2,0},{3,1},{4,6},{5,7},{6,4},{7,5},{8,10},{9,11},{10,... | collective-permute-start | bytes 294920 | tf_op jit(solution)/shard_map/ppermute | solution.py:475
  28.9 1.9 %collective-permute-start.7 = (f32[2,3,32,128]{3,2,1,0:T(8,128)S(1)}, f32[2,3,32,128]{3,2,1,0:T(8,128)S(1)}, u32[]{:S(2)}, u32[]{:S(2)}) collective-permute-start(f32[2,3,32,128]{3,2,1,0:T(8,128)S(1)} %pad_maximum_fusion.5), channel_id=1, source_target_pairs={{0,10},{1,11},{2,8},{3,9},{4,14},{5,15},{6,12},{7,13},{8,2},{9,3},... | collective-permute-start | bytes 294920 | tf_op jit(solution)/shard_map/ppermute | solution.py:475
  30.8 3.3 %collective-permute-done.3 = f32[2,3,32,128]{3,2,1,0:T(8,128)S(1)} collective-permute-done((f32[2,3,32,128]{3,2,1,0:T(8,128)S(1)}, f32[2,3,32,128]{3,2,1,0:T(8,128)S(1)}, u32[]{:S(2)}, u32[]{:S(2)}) %collective-permute-start.3) | collective-permute-done | bytes 98336 | tf_op jit(solution)/shard_map/ppermute | solution.py:475
  34.0 1.8 %collective-permute-start.8 = (f32[2,3,32,128]{3,2,1,0:T(8,128)S(1)}, f32[2,3,32,128]{3,2,1,0:T(8,128)S(1)}, u32[]{:S(2)}, u32[]{:S(2)}) collective-permute-start(f32[2,3,32,128]{3,2,1,0:T(8,128)S(1)} %pad_maximum_fusion.6), channel_id=1, source_target_pairs={{0,12},{1,13},{2,14},{3,15},{4,8},{5,9},{6,10},{7,11},{8,4},{9,5},... | collective-permute-start | bytes 294920 | tf_op jit(solution)/shard_map/ppermute | solution.py:475
  35.8 0.0 collective-permute-done.4
  35.8 2.0 %collective-permute-start.9 = (f32[2,3,32,128]{3,2,1,0:T(8,128)S(1)}, f32[2,3,32,128]{3,2,1,0:T(8,128)S(1)}, u32[]{:S(2)}, u32[]{:S(2)}) collective-permute-start(f32[2,3,32,128]{3,2,1,0:T(8,128)S(1)} %pad_maximum_fusion.7), channel_id=1, source_target_pairs={{0,14},{1,15},{2,12},{3,13},{4,10},{5,11},{6,8},{7,9},{8,6},{9,7},... | collective-permute-start | bytes 294920 | tf_op jit(solution)/shard_map/ppermute | solution.py:475
  37.8 0.0 collective-permute-done.5
  37.8 0.0 collective-permute-done.6
  37.9 0.3 collective-permute-done.7
  38.2 2.9 %collective-permute-done.8 = f32[2,3,32,128]{3,2,1,0:T(8,128)S(1)} collective-permute-done((f32[2,3,32,128]{3,2,1,0:T(8,128)S(1)}, f32[2,3,32,128]{3,2,1,0:T(8,128)S(1)}, u32[]{:S(2)}, u32[]{:S(2)}) %collective-permute-start.8) | collective-permute-done | bytes 98336 | tf_op jit(solution)/shard_map/ppermute | solution.py:475
  41.1 2.3 %collective-permute-done.9 = f32[2,3,32,128]{3,2,1,0:T(8,128)S(1)} collective-permute-done((f32[2,3,32,128]{3,2,1,0:T(8,128)S(1)}, f32[2,3,32,128]{3,2,1,0:T(8,128)S(1)}, u32[]{:S(2)}, u32[]{:S(2)}) %collective-permute-start.9) | collective-permute-done | bytes 98336 | tf_op jit(solution)/shard_map/ppermute | solution.py:475
  43.3 1.3 %combine.1 = f32[512,128]{1,0:T(8,128)} custom-call(f32[16,48]{1,0:T(8,128)S(1)} %copy.14.adjoint_ref, f32[32,16,128]{2,1,0:T(8,128)S(1)} %estimate_part.1.estimate_ref, f32[1536,128]{1,0:T(8,128)S(1)} %bitcast.40), custom_call_target="tpu_custom_call" | custom-call | flops 6291456 | bytes 786432 | tf_op jit(solution)/shard_map/combine/pallas_call | solution.py:402
  (22 shorter events, 0.2 us)
Async XLA Ops:
  0.0 13.2 %copy-start.6 = (f32[16,16]{0,1:T(8,128)S(1)}, f32[16,16]{0,1:T(8,128)}, u32[]{:S(2)}) copy-start(f32[16,16]{0,1:T(8,128)} %constant.93.clone) | copy-start | bytes 3076
  0.0 13.2 %copy-start.7 = (f32[16,16]{0,1:T(8,128)S(1)}, f32[16,16]{0,1:T(8,128)}, u32[]{:S(2)}) copy-start(f32[16,16]{0,1:T(8,128)} %constant.94.clone) | copy-start | bytes 3076
  0.0 6.6 %copy-start.3 = (f32[16,32,128]{2,1,0:T(8,128)S(1)}, f32[16,32,128]{2,1,0:T(8,128)}, u32[]{:S(2)}) copy-start(f32[16,32,128]{2,1,0:T(8,128)} %param.10) | copy-start | bytes 786436
  0.0 13.0 %copy-start.8 = (f32[3,2,16]{2,1,0:T(2,128)S(1)}, f32[3,2,16]{2,1,0:T(2,128)}, u32[]{:S(2)}) copy-start(f32[3,2,16]{2,1,0:T(2,128)} %param.13) | copy-start | bytes 1156
  6.1 18.4 %collective-permute-start.2 = (f32[8,3,32,128]{3,2,1,0:T(8,128)}, f32[8,3,32,128]{3,2,1,0:T(8,128)S(1)}, u32[]{:S(2)}, u32[]{:S(2)}) collective-permute-start(f32[8,3,32,128]{3,2,1,0:T(8,128)} %get-tuple-element.14), channel_id=1, source_target_pairs={{0,1},{1,0},{2,3},{3,2},{4,5},{5,4},{6,7},{7,6},{8,9},{9,8},{10,11... | collective-permute-start | bytes 1179656 | tf_op jit(solution)/shard_map/ppermute | solution.py:463
  7.3 10.2 %collective-permute-start = (f32[16,6,128]{2,1,0:T(8,128)}, f32[16,6,128]{2,1,0:T(8,128)}, u32[]{:S(2)}, u32[]{:S(2)}) collective-permute-start(f32[16,6,128]{2,1,0:T(8,128)} %get-tuple-element.31), channel_id=1, source_target_pairs={{0,1},{1,2},{2,3},{3,4},{4,5},{5,6},{6,7},{7,8},{8,9},{9,10},{10,1... | collective-permute-start | bytes 147464 | tf_op jit(solution)/shard_map/ppermute | solution.py:426
  7.3 10.2 %collective-permute-start.1 = (f32[16,6,128]{2,1,0:T(8,128)}, f32[16,6,128]{2,1,0:T(8,128)}, u32[]{:S(2)}, u32[]{:S(2)}) collective-permute-start(f32[16,6,128]{2,1,0:T(8,128)} %get-tuple-element.32), channel_id=1, source_target_pairs={{0,15},{1,0},{2,1},{3,2},{4,3},{5,4},{6,5},{7,6},{8,7},{9,8},{10,9... | collective-permute-start | bytes 147464 | tf_op jit(solution)/shard_map/ppermute | solution.py:427
  13.4 6.8 %copy-start = (f32[6,528,128]{2,1,0:T(8,128)S(1)}, f32[6,528,128]{2,1,0:T(8,128)}, u32[]{:S(2)}) copy-start(f32[6,528,128]{2,1,0:T(8,128)} %constant.91.clone.table_hbm) | copy-start | bytes 4866052
  13.4 6.8 %copy-start.1 = (f32[3,128,128]{2,1,0:T(8,128)S(1)}, f32[3,128,128]{2,1,0:T(8,128)}, u32[]{:S(2)}) copy-start(f32[3,128,128]{2,1,0:T(8,128)} %blur_ref.1) | copy-start | bytes 589828
  13.5 6.8 %copy-start.2 = (f32[3,7]{1,0:T(4,128)S(1)}, f32[3,7]{1,0:T(4,128)}, u32[]{:S(2)}) copy-start(f32[3,7]{1,0:T(4,128)} %taps_ref.1) | copy-start | bytes 256
  20.2 4.3 %copy-start.5 = (f32[3,32,128]{2,1,0:T(8,128)S(1)}, f32[3,32,128]{2,1,0:T(8,128)}, u32[]{:S(2)}) copy-start(f32[3,32,128]{2,1,0:T(8,128)} %get-tuple-element.18) | copy-start | bytes 147460
  20.2 4.9 %copy-start.4 = (f32[1,3,32,128]{3,2,1,0:T(8,128)S(1)}, f32[1,3,32,128]{3,2,1,0:T(8,128)}, u32[]{:S(2)}) copy-start(f32[1,3,32,128]{3,2,1,0:T(8,128)} %get-tuple-element.19) | copy-start | bytes 147460
  24.5 13.3 %collective-permute-start.6 = (f32[2,3,32,128]{3,2,1,0:T(8,128)S(1)}, f32[2,3,32,128]{3,2,1,0:T(8,128)S(1)}, u32[]{:S(2)}, u32[]{:S(2)}) collective-permute-start(f32[2,3,32,128]{3,2,1,0:T(8,128)S(1)} %pad_maximum_fusion.4), channel_id=1, source_target_pairs={{0,8},{1,9},{2,10},{3,11},{4,12},{5,13},{6,14},{7,15},{8,0},{9,1},... | collective-permute-start | bytes 294920 | tf_op jit(solution)/shard_map/ppermute | solution.py:475
  25.2 12.6 %collective-permute-start.5 = (f32[2,3,32,128]{3,2,1,0:T(8,128)S(1)}, f32[2,3,32,128]{3,2,1,0:T(8,128)S(1)}, u32[]{:S(2)}, u32[]{:S(2)}) collective-permute-start(f32[2,3,32,128]{3,2,1,0:T(8,128)S(1)} %pad_maximum_fusion.3), channel_id=1, source_target_pairs={{0,6},{1,7},{2,4},{3,5},{4,2},{5,3},{6,0},{7,1},{8,14},{9,15},{10,... | collective-permute-start | bytes 294920 | tf_op jit(solution)/shard_map/ppermute | solution.py:475
  26.9 8.9 %collective-permute-start.4 = (f32[2,3,32,128]{3,2,1,0:T(8,128)S(1)}, f32[2,3,32,128]{3,2,1,0:T(8,128)S(1)}, u32[]{:S(2)}, u32[]{:S(2)}) collective-permute-start(f32[2,3,32,128]{3,2,1,0:T(8,128)S(1)} %pad_maximum_fusion.2), channel_id=1, source_target_pairs={{0,4},{1,5},{2,6},{3,7},{4,0},{5,1},{6,2},{7,3},{8,12},{9,13},{10,... | collective-permute-start | bytes 294920 | tf_op jit(solution)/shard_map/ppermute | solution.py:475
  27.4 6.6 %collective-permute-start.3 = (f32[2,3,32,128]{3,2,1,0:T(8,128)S(1)}, f32[2,3,32,128]{3,2,1,0:T(8,128)S(1)}, u32[]{:S(2)}, u32[]{:S(2)}) collective-permute-start(f32[2,3,32,128]{3,2,1,0:T(8,128)S(1)} %pad_maximum_fusion.1), channel_id=1, source_target_pairs={{0,2},{1,3},{2,0},{3,1},{4,6},{5,7},{6,4},{7,5},{8,10},{9,11},{10,... | collective-permute-start | bytes 294920 | tf_op jit(solution)/shard_map/ppermute | solution.py:475
  28.9 9.3 %collective-permute-start.7 = (f32[2,3,32,128]{3,2,1,0:T(8,128)S(1)}, f32[2,3,32,128]{3,2,1,0:T(8,128)S(1)}, u32[]{:S(2)}, u32[]{:S(2)}) collective-permute-start(f32[2,3,32,128]{3,2,1,0:T(8,128)S(1)} %pad_maximum_fusion.5), channel_id=1, source_target_pairs={{0,10},{1,11},{2,8},{3,9},{4,14},{5,15},{6,12},{7,13},{8,2},{9,3},... | collective-permute-start | bytes 294920 | tf_op jit(solution)/shard_map/ppermute | solution.py:475
  34.0 7.0 %collective-permute-start.8 = (f32[2,3,32,128]{3,2,1,0:T(8,128)S(1)}, f32[2,3,32,128]{3,2,1,0:T(8,128)S(1)}, u32[]{:S(2)}, u32[]{:S(2)}) collective-permute-start(f32[2,3,32,128]{3,2,1,0:T(8,128)S(1)} %pad_maximum_fusion.6), channel_id=1, source_target_pairs={{0,12},{1,13},{2,14},{3,15},{4,8},{5,9},{6,10},{7,11},{8,4},{9,5},... | collective-permute-start | bytes 294920 | tf_op jit(solution)/shard_map/ppermute | solution.py:475
  35.8 7.5 %collective-permute-start.9 = (f32[2,3,32,128]{3,2,1,0:T(8,128)S(1)}, f32[2,3,32,128]{3,2,1,0:T(8,128)S(1)}, u32[]{:S(2)}, u32[]{:S(2)}) collective-permute-start(f32[2,3,32,128]{3,2,1,0:T(8,128)S(1)} %pad_maximum_fusion.7), channel_id=1, source_target_pairs={{0,14},{1,15},{2,12},{3,13},{4,10},{5,11},{6,8},{7,9},{8,6},{9,7},... | collective-permute-start | bytes 294920 | tf_op jit(solution)/shard_map/ppermute | solution.py:475
